TPU v7x, 32 devices: a whole 2x2x4 slice. The times are simulated.
32 devices in a mesh: dp: 16 (over z, y, x), tensor: 2 (over core).
Axes of the slice: x: 2, y: 2, z: 4, core: 2. Of those that a mesh axis runs over, the one named last changes fastest.
Arguments:
- tokens: bfloat16 [8192, 768], P('dp'), may hold values from -6 to 6
- segments: int32 [8192], P('dp'), may hold values from 0 to 8191, as said below
- routes: int32 [8192, 2], P('dp'), may hold values from 0 to 7, as said below
- prev_logits: float32 [8192, 8], P('dp'), may hold values from -3 to 3
- attn_gain: float32 [768], replicated, may hold values from 0.5 to 1.5
- w_qkv: bfloat16 [3, 768, 768], P(None, None, 'tensor'), may hold values from -0.21875 to 0.21875
- w_out: bfloat16 [768, 768], P('tensor'), may hold values from -1.75 to 1.75
- ffn_gain: float32 [768], replicated, may hold values from 0.5 to 1.5
- w_router: bfloat16 [768, 8], replicated, may hold values from -0.109375 to 0.109375
- w_const: bfloat16 [768, 4], replicated, may hold values from -0.21875 to 0.21875
- v_const: float32 [2, 768], replicated, may hold values from -6 to 6
- w_gu: bfloat16 [4, 2, 768, 2048], P(None, None, None, 'tensor'), may hold values from -0.21875 to 0.21875
- w_down: bfloat16 [4, 2048, 768], P(None, 'tensor'), may hold values from -0.75 to 0.75
- cotangent: bfloat16 [8192, 768], P('dp'), may hold values from -6 to 6
Outputs:
- output: bfloat16 [8192, 768], P('dp')
- tokens_grad: float32 [8192, 768], P('dp')
- prev_grad: float32 [8192, 8], P('dp')
- attn_gain_grad: float32 [768], P('dp')
- w_qkv_grad: float32 [3, 768, 768], P(None, 'dp', 'tensor')
- w_out_grad: float32 [768, 768], P('tensor', 'dp')
- ffn_gain_grad: float32 [768], P('dp')
- w_router_grad: float32 [768, 8], P('dp')
- w_const_grad: float32 [768, 4], P('dp')
- v_const_grad: float32 [2, 768], P(None, 'dp')
- w_gu_grad: float32 [4, 2, 768, 2048], P(None, None, 'dp', 'tensor')
- w_down_grad: float32 [4, 2048, 768], P(None, 'tensor', 'dp')
Inputs may be any that keep to these rules, and one draw needn't show every extreme that they name: `segments`: ids are non-decreasing along the tokens, and tokens of different packed sequences of 8192 tokens have different ids. `routes`: a token's two experts differ, and the first is a feed-forward expert, a number below 4.
All inputs are finite; a program needn't handle non-finite values.
Results may differ from a plain program's by a relative error of at most 0.019.
Values may be sent and summed in bfloat16 or wider, within the bound.
No kernel may reach another device: no remote copies, remote signals or barrier semaphores. Data moves between devices by JAX's collectives and lax.ppermute only.
A program may use at most 448 MiB of HBM per device.

v0:
```python
import math

import jax
import jax.numpy as jnp
from jax import lax
from jax.sharding import PartitionSpec as P

HD = 64
E_FFN = 4
NCONST = 2
E_ALL = 8
TOP = 2
BLOCK = 128
SPAN = 16
SEQ_LEN = 8192


EPSILON = 1e-05
HIGHEST = lax.Precision.HIGHEST


def passed_along(block, axis, distance):
    devices = range(lax.axis_size(axis))
    route = [(i - distance, i) for i in devices if i - distance in devices]
    return lax.ppermute(block, axis, route)


def norm_forward(values, gain_vec):
    inverse = lax.rsqrt(jnp.mean(values * values, axis=-1, keepdims=True) + EPSILON)
    return (values * inverse * gain_vec, inverse)


def norm_backward(values, inverse, gain_vec, upstream):
    scaled = upstream * gain_vec
    inner_mean = jnp.mean(scaled * values, axis=-1, keepdims=True)
    return (
        inverse * scaled - values * inverse * inverse * inverse * inner_mean,
        jnp.sum(upstream * values * inverse, axis=0),
    )


def rotary_tables(global_index, half_dim):
    position = (global_index % SEQ_LEN).astype(jnp.float32)
    inv_freq = jnp.exp(jnp.arange(half_dim).astype(jnp.float32) * (-math.log(10000.0) / half_dim))
    phases = position[:, None] * inv_freq[None, :]
    return (jnp.cos(phases)[:, None, :], jnp.sin(phases)[:, None, :])


def rotate(values, cosine_table, sine_table):
    half_dim = values.shape[-1] // 2
    first_half = values[..., :half_dim]
    second_half = values[..., half_dim:]
    return jnp.concatenate(
        [
            first_half * cosine_table - second_half * sine_table,
            second_half * cosine_table + first_half * sine_table,
        ],
        axis=-1,
    )


def unrotate(grads_in, cosine_table, sine_table):
    half_dim = grads_in.shape[-1] // 2
    first_half = grads_in[..., :half_dim]
    second_half = grads_in[..., half_dim:]
    return jnp.concatenate(
        [
            first_half * cosine_table + second_half * sine_table,
            second_half * cosine_table - first_half * sine_table,
        ],
        axis=-1,
    )


def block_expon(queries, key_block, allowed, inverse_root):
    raw_scores = (
        jnp.einsum("qhd,khd->hqk", queries, key_block, preferred_element_type=jnp.float32)
        * inverse_root
    )
    return jnp.where(allowed[None], jnp.exp(jnp.where(allowed[None], raw_scores, 0.0)), 0.0)


def local(
    tokens,
    segments,
    routes,
    prev_logits,
    attn_gain,
    w_qkv,
    w_out,
    ffn_gain,
    w_router,
    w_const,
    v_const,
    w_gu,
    w_down,
    cotangent,
):
    tok_count = tokens.shape[0]
    model_width = tokens.shape[1]
    head_count = w_qkv.shape[2] // HD
    inverse_root = 1.0 / math.sqrt(HD)
    my_index = lax.axis_index("dp")
    group_pos = my_index % SPAN
    global_index = my_index * tok_count + jnp.arange(tok_count, dtype=jnp.int32)
    cosine_table, sine_table = rotary_tables(global_index, HD // 2)
    inputs_f32 = tokens.astype(jnp.float32)
    normed_attn, inverse_attn = norm_forward(inputs_f32, attn_gain)
    normed_attn_low = normed_attn.astype(jnp.bfloat16)
    qkv_proj = jnp.einsum("td,sdf->stf", normed_attn_low, w_qkv, preferred_element_type=jnp.float32)
    shaped = (tok_count, head_count, HD)
    queries = rotate(qkv_proj[0].reshape(shaped), cosine_table, sine_table).astype(jnp.bfloat16)
    keys_rot = rotate(qkv_proj[1].reshape(shaped), cosine_table, sine_table).astype(jnp.bfloat16)
    values_low = qkv_proj[2].reshape(shaped).astype(jnp.bfloat16)
    key_blocks = [(keys_rot, values_low, segments, global_index, jnp.array(True))]
    for distance in range(1, SPAN):
        moved_keys, moved_values, moved_segs = passed_along(
            (keys_rot, values_low, segments), "dp", distance
        )
        key_blocks.append(
            (
                moved_keys,
                moved_values,
                moved_segs,
                global_index - distance * tok_count,
                group_pos >= distance,
            )
        )
    mask_list = []
    for key_block, value_block, seg_block, index_block, same_seq in key_blocks:
        mask_list.append(
            (segments[:, None] == seg_block[None, :])
            & (index_block[None, :] <= global_index[:, None])
            & same_seq
        )
    totals = jnp.zeros((head_count, tok_count), jnp.float32)
    for distance in range(SPAN):
        totals = totals + jnp.sum(
            block_expon(queries, key_blocks[distance][0], mask_list[distance], inverse_root),
            axis=-1,
        )
    heads_out = jnp.zeros(shaped, jnp.float32)
    for distance in range(SPAN):
        weighted_weights_now = (
            block_expon(queries, key_blocks[distance][0], mask_list[distance], inverse_root)
            / totals[..., None]
        )
        heads_out = heads_out + jnp.einsum(
            "hqk,khd->qhd",
            weighted_weights_now.astype(jnp.bfloat16),
            key_blocks[distance][1],
            preferred_element_type=jnp.float32,
        )
    heads_low = heads_out.reshape(tok_count, -1).astype(jnp.bfloat16)
    branch_part = jnp.dot(heads_low, w_out, preferred_element_type=jnp.float32)
    branch = lax.psum(branch_part.astype(jnp.bfloat16), "tensor").astype(jnp.float32)
    residual = inputs_f32 + branch
    normed_ffn, inverse_ffn = norm_forward(residual, ffn_gain)
    normed_low = normed_ffn.astype(jnp.bfloat16)
    logits = jnp.dot(normed_low, w_router, preferred_element_type=jnp.float32) + prev_logits
    router_probs = jax.nn.softmax(logits, axis=-1)
    route_hot = (routes[:, :, None] == jnp.arange(E_ALL, dtype=jnp.int32)[None, None, :]).astype(
        jnp.float32
    )
    gating = jnp.sum(route_hot * router_probs[:, None, :], axis=-1)
    expert_weight = jnp.sum(route_hot * gating[:, :, None], axis=1)
    const_logits = jnp.dot(normed_low, w_const, preferred_element_type=jnp.float32).reshape(
        tok_count, NCONST, 2
    )
    blend_weights = jax.nn.softmax(const_logits, axis=-1)
    const_out = (
        blend_weights[..., 0:1] * normed_ffn[:, None, :] + blend_weights[..., 1:2] * v_const[None]
    )
    flat_expert = routes.reshape(-1)
    route_total = flat_expert.shape[0]
    is_ffn = flat_expert < E_FFN
    expert_hot = (flat_expert[:, None] == jnp.arange(E_FFN, dtype=jnp.int32)[None, :]).astype(
        jnp.int32
    )
    counts = jnp.sum(expert_hot, axis=0)
    padded = (counts + BLOCK - 1) // BLOCK * BLOCK
    block_ends = jnp.cumsum(padded)
    starts = block_ends - padded
    ranking = jnp.sum((jnp.cumsum(expert_hot, axis=0) - 1) * expert_hot, axis=1)
    row_count = route_total + E_FFN * BLOCK
    block_count = row_count // BLOCK
    row_slots = jnp.where(
        is_ffn, jnp.sum(expert_hot * starts[None, :], axis=1) + ranking, row_count
    )
    flat_token = jnp.arange(route_total, dtype=jnp.int32) // TOP
    row_token = jnp.zeros((row_count,), jnp.int32).at[row_slots].set(flat_token, mode="drop")
    row_gate = (
        jnp.zeros((row_count,), jnp.float32).at[row_slots].set(gating.reshape(-1), mode="drop")
    )
    row_live = jnp.zeros((row_count,), jnp.bool_).at[row_slots].set(True, mode="drop")
    block_first = jnp.arange(block_count, dtype=jnp.int32) * BLOCK
    block_expert = jnp.minimum(
        jnp.sum((block_ends[None, :] <= block_first[:, None]).astype(jnp.int32), axis=1), E_FFN - 1
    )
    block_used = block_first < block_ends[-1]
    rows_in = jnp.where(
        row_live[:, None], normed_low[row_token], jnp.zeros((), jnp.bfloat16)
    ).reshape(block_count, BLOCK, model_width)

    def expert_forward(operand):
        block_rows, expert_id = operand
        gate_up = lax.dynamic_index_in_dim(w_gu, expert_id, 0, keepdims=False)
        down_proj = lax.dynamic_index_in_dim(w_down, expert_id, 0, keepdims=False)
        both_parts = jnp.einsum(
            "rd,sdf->srf", block_rows, gate_up, preferred_element_type=jnp.float32
        )
        hidden = (jax.nn.silu(both_parts[0]) * both_parts[1]).astype(jnp.bfloat16)
        return (jnp.dot(hidden, down_proj, preferred_element_type=jnp.float32), both_parts, hidden)

    def expert_step(operand):
        return expert_forward((operand[0], operand[1]))

    expert_rows_out, kept_both, kept_hidden = lax.map(
        expert_step, (rows_in, block_expert, block_used)
    )
    safe_slots = jnp.minimum(row_slots, row_count - 1)
    route_out = jnp.where(
        is_ffn[:, None], expert_rows_out.reshape(row_count, model_width)[safe_slots], 0.0
    ).reshape(tok_count, TOP, model_width)
    ffn_part = jnp.sum(gating[:, :, None] * route_out, axis=1)
    ffn_sum = lax.psum(ffn_part.astype(jnp.bfloat16), "tensor").astype(jnp.float32)
    copy_weight = expert_weight[:, E_FFN + 1 : E_FFN + 2]
    const_weight = expert_weight[:, E_FFN + 2 :]
    mixture = (
        residual
        + ffn_sum
        + copy_weight * normed_ffn
        + jnp.sum(const_weight[:, :, None] * const_out, axis=1)
    )
    output = mixture.astype(jnp.bfloat16)
    upstream = cotangent.astype(jnp.float32)
    expert_cot = (
        (row_gate[:, None] * upstream[row_token])
        .astype(jnp.bfloat16)
        .reshape(block_count, BLOCK, model_width)
    )

    def expert_grad(operand):
        cot_rows, block_rows, both_parts, hidden, expert_id = operand
        gate_up = lax.dynamic_index_in_dim(w_gu, expert_id, 0, keepdims=False)
        down_proj = lax.dynamic_index_in_dim(w_down, expert_id, 0, keepdims=False)
        hidden_grad = jnp.einsum(
            "rd,fd->rf", cot_rows, down_proj, preferred_element_type=jnp.float32
        )
        sigmoid_gate = jax.nn.sigmoid(both_parts[0])
        gate_grad = (
            hidden_grad
            * both_parts[1]
            * sigmoid_gate
            * (1.0 + both_parts[0] * (1.0 - sigmoid_gate))
        )
        up_grad = hidden_grad * both_parts[0] * sigmoid_gate
        both_grad = jnp.stack([gate_grad, up_grad]).astype(jnp.bfloat16)
        down_step = jnp.einsum("rf,rd->fd", hidden, cot_rows, preferred_element_type=jnp.float32)
        gu_step = jnp.einsum(
            "rd,srf->sdf", block_rows, both_grad, preferred_element_type=jnp.float32
        )
        row_grad = jnp.einsum("srf,sdf->rd", both_grad, gate_up, preferred_element_type=jnp.float32)
        return (row_grad, gu_step, down_step)

    def grad_scan(carried, operand):
        gu_total, down_total = carried
        row_grad, gu_step, down_step = expert_grad(operand[:5])
        gu_total = gu_total.at[operand[4]].add(gu_step)
        down_total = down_total.at[operand[4]].add(down_step)
        return ((gu_total, down_total), row_grad)

    (w_gu_local, w_down_local), rows_grad = lax.scan(
        grad_scan,
        (jnp.zeros(w_gu.shape, jnp.float32), jnp.zeros(w_down.shape, jnp.float32)),
        (expert_cot, rows_in, kept_both, kept_hidden, block_expert, block_used),
    )
    route_grad = jnp.where(
        is_ffn[:, None], rows_grad.reshape(row_count, model_width)[safe_slots], 0.0
    ).reshape(tok_count, TOP, model_width)
    normed_part = jnp.sum(route_grad, axis=1)
    gating_part = jnp.sum(upstream[:, None, :] * route_out, axis=-1)
    normed_ffn_grad, gating_ffn = (
        lax.psum(normed_part.astype(jnp.bfloat16), "tensor").astype(jnp.float32),
        lax.psum(gating_part.astype(jnp.bfloat16), "tensor").astype(jnp.float32),
    )
    copy_dot = jnp.sum(upstream * normed_ffn, axis=-1)
    const_dot = jnp.sum(upstream[:, None, :] * const_out, axis=-1)
    local_dots = jnp.concatenate(
        [jnp.zeros((tok_count, E_FFN + 1), jnp.float32), copy_dot[:, None], const_dot], axis=1
    )
    gating_grad = gating_ffn + jnp.sum(route_hot * local_dots[:, None, :], axis=-1)
    probs_grad = jnp.sum(route_hot * gating_grad[:, :, None], axis=1)
    prev_grad = router_probs * (
        probs_grad - jnp.sum(router_probs * probs_grad, axis=-1, keepdims=True)
    )
    normed_f32 = normed_low.astype(jnp.float32)
    router_grad = jnp.einsum("td,te->de", normed_f32, prev_grad, precision=HIGHEST)
    upstream_const = jnp.dot(upstream, v_const.T, precision=HIGHEST)
    blend_grad = jnp.stack(
        [const_weight * copy_dot[:, None], const_weight * upstream_const], axis=-1
    )
    const_logit_grad = blend_weights * (
        blend_grad - jnp.sum(blend_weights * blend_grad, axis=-1, keepdims=True)
    )
    const_logit_flat = const_logit_grad.reshape(tok_count, 2 * NCONST)
    const_grad = jnp.einsum("td,tc->dc", normed_f32, const_logit_flat, precision=HIGHEST)
    v_const_local = jnp.einsum(
        "tc,td->cd", const_weight * blend_weights[..., 1], upstream, precision=HIGHEST
    )
    normed_grad = normed_ffn_grad + jnp.dot(
        prev_grad, w_router.astype(jnp.float32).T, precision=HIGHEST
    )
    normed_grad = normed_grad + jnp.dot(
        const_logit_flat, w_const.astype(jnp.float32).T, precision=HIGHEST
    )
    normed_grad = (
        normed_grad
        + (copy_weight + jnp.sum(const_weight * blend_weights[..., 0], axis=1, keepdims=True))
        * upstream
    )
    residual_norm_grad, ffn_gain_local = norm_backward(residual, inverse_ffn, ffn_gain, normed_grad)
    residual_grad = upstream + residual_norm_grad
    branch_cot = residual_grad.astype(jnp.bfloat16)
    out_grad_local = jnp.einsum(
        "tf,td->fd", heads_low, branch_cot, preferred_element_type=jnp.float32
    )
    heads_cot = (
        jnp.einsum("td,fd->tf", branch_cot, w_out, preferred_element_type=jnp.float32)
        .astype(jnp.bfloat16)
        .reshape(shaped)
    )
    delta_rows = jnp.transpose(jnp.sum(heads_cot.astype(jnp.float32) * heads_out, axis=-1))
    zero_heads = jnp.zeros(shaped, jnp.float32)
    query_grad = zero_heads
    key_grad = zero_heads
    value_grad = zero_heads
    for distance in range(SPAN):
        block_key_in = key_blocks[distance][0]
        block_value_in = key_blocks[distance][1]
        block_allowed = mask_list[distance]
        weights_now = (
            block_expon(queries, block_key_in, block_allowed, inverse_root) / totals[..., None]
        )
        value_step = jnp.einsum(
            "hqk,qhd->khd",
            weights_now.astype(jnp.bfloat16),
            heads_cot,
            preferred_element_type=jnp.float32,
        )
        prob_grad = jnp.einsum(
            "qhd,khd->hqk", heads_cot, block_value_in, preferred_element_type=jnp.float32
        )
        score_grad = (weights_now * (prob_grad - delta_rows[..., None])).astype(jnp.bfloat16)
        block_value_step = value_step
        query_step = (
            jnp.einsum("hqk,khd->qhd", score_grad, block_key_in, preferred_element_type=jnp.float32)
            * inverse_root
        )
        key_step = (
            jnp.einsum("hqk,qhd->khd", score_grad, queries, preferred_element_type=jnp.float32)
            * inverse_root
        )
        query_step, key_step, value_step = (query_step, key_step, block_value_step)
        query_grad = query_grad + query_step
        if distance == 0:
            key_grad = key_step
            value_grad = value_step
        else:
            back_keys, back_values = (
                passed_along(key_step.astype(jnp.bfloat16), "dp", -distance).astype(key_step.dtype),
                passed_along(value_step.astype(jnp.bfloat16), "dp", -distance).astype(
                    value_step.dtype
                ),
            )
            key_grad = key_grad + back_keys
            value_grad = value_grad + back_values
    qkv_grad = (
        jnp.stack(
            [
                unrotate(query_grad, cosine_table, sine_table),
                unrotate(key_grad, cosine_table, sine_table),
                value_grad,
            ]
        )
        .reshape(3, tok_count, -1)
        .astype(jnp.bfloat16)
    )
    qkv_grad_local = jnp.einsum(
        "td,stf->sdf", normed_attn_low, qkv_grad, preferred_element_type=jnp.float32
    )
    attn_norm_part = jnp.einsum("stf,sdf->td", qkv_grad, w_qkv, preferred_element_type=jnp.float32)
    attn_norm_grad = lax.psum(attn_norm_part.astype(jnp.bfloat16), "tensor").astype(jnp.float32)
    token_norm_grad, attn_gain_local = norm_backward(
        inputs_f32, inverse_attn, attn_gain, attn_norm_grad
    )
    tokens_grad = residual_grad + token_norm_grad
    (
        attn_gain_grad,
        w_qkv_grad,
        w_out_grad,
        ffn_gain_grad,
        w_router_grad,
        w_const_grad,
        v_const_grad,
        w_gu_grad,
        w_down_grad,
    ) = (
        lax.psum_scatter(attn_gain_local, "dp", scatter_dimension=0, tiled=True),
        lax.psum_scatter(qkv_grad_local, "dp", scatter_dimension=1, tiled=True),
        lax.psum_scatter(out_grad_local, "dp", scatter_dimension=1, tiled=True),
        lax.psum_scatter(ffn_gain_local, "dp", scatter_dimension=0, tiled=True),
        lax.psum_scatter(router_grad, "dp", scatter_dimension=0, tiled=True),
        lax.psum_scatter(const_grad, "dp", scatter_dimension=0, tiled=True),
        lax.psum_scatter(v_const_local, "dp", scatter_dimension=1, tiled=True),
        lax.psum_scatter(w_gu_local, "dp", scatter_dimension=2, tiled=True),
        lax.psum_scatter(w_down_local, "dp", scatter_dimension=2, tiled=True),
    )
    return (
        output,
        tokens_grad,
        prev_grad,
        attn_gain_grad,
        w_qkv_grad,
        w_out_grad,
        ffn_gain_grad,
        w_router_grad,
        w_const_grad,
        v_const_grad,
        w_gu_grad,
        w_down_grad,
    )


def solution(mesh):
    return jax.shard_map(
        local,
        mesh=mesh,
        in_specs=(
            P("dp", None),
            P("dp"),
            P("dp", None),
            P("dp", None),
            P(),
            P(None, None, "tensor"),
            P("tensor", None),
            P(),
            P(),
            P(),
            P(),
            P(None, None, None, "tensor"),
            P(None, "tensor", None),
            P("dp", None),
        ),
        out_specs=(
            P("dp", None),
            P("dp", None),
            P("dp", None),
            P("dp"),
            P(None, "dp", "tensor"),
            P("tensor", "dp"),
            P("dp"),
            P("dp", None),
            P("dp", None),
            P(None, "dp"),
            P(None, None, "dp", "tensor"),
            P(None, "tensor", "dp"),
        ),
        check_vma=False,
    )
```

profile of v0, /device:TPU:17, one launch (start us, length us, event | category | flops | bytes accessed | tf_op | source)
XLA Modules:
  0.0 3047.6 jit_solution(9471674040563756191)
XLA Ops:
  88.3 17.7 collective-permute-done.1
  133.1 17.3 collective-permute-start.7
  183.8 14.6 collective-permute-done.13
  204.3 22.7 collective-permute-done.15
  256.6 10.5 collective-permute-start.31
  276.5 17.1 collective-permute-done.31
  293.6 22.8 collective-permute-start.32
  321.6 11.2 collective-permute-start.33
  352.8 7.0 collective-permute-done.35
  365.0 21.0 collective-permute-done.36
  390.2 16.0 collective-permute-done.37
  416.9 9.2 collective-permute-start.30
  452.8 91.6 %all-reduce.10.cloned.1.call-done = bf16[512,768]{1,0:T(8,128)(2,1)} async-done(((bf16[512,768]{1,0:T(8,128)(2,1)}), bf16[512,768]{1,0:T(8,128)(2,1)}) %all-reduce.10.cloned.1.call-update) | async-done | bytes 786448 | tf_op jit(solution)/shard_map/psum | solution.py:156
  556.8 7.9 gather_fusion
  568.4 10.2 multiply_reduce_fusion
  585.7 118.1 %while.30 = (s32[]{:T(128)}, f32[12,128,768]{2,1,0:T(8,128)}, f32[12,2,128,1024]{2,3,1,0:T(8,128)}, bf16[12,128,1024]{1,2,0:T(8,128)(2,1)}, s32[12]{0:T(128)S(1)...) while((s32[]{:T(128)}, f32[12,128,768]{2,1,0:T(8,128)}, ...), condition=%wide.region_32.33_spmd, body=%wide.region_31.32_spmd.sunk | while | flops 604766208 | bytes 9242287 | solution.py:218
  703.8 8.2 gather_fusion.1
  741.4 11.5 broadcast_in_dim.791.clone
  753.0 751.8 %while.31 = (s32[]{:T(128)}, f32[4,2,768,1024]{3,2,1,0:T(8,128)}, f32[4,1024,768]{1,2,0:T(8,128)}, f32[12,128,768]{2,1,0:T(8,128)}, s32[12]{0:T(128)S(1)}, /*ind...) while((s32[]{:T(128)}, f32[4,2,768,1024]{3,2,1,0:T(8,128)}, ...), condition=%wide.region_43.44_spmd, body=%wide.region_40.43_spmd.sunk | while | flops 1214906368 | bytes 132321624 | solution.py:273
  794.5 7.2 add_select_fusion.6
  801.7 6.7 copy.720
  857.2 7.2 add_select_fusion.6
  864.4 6.7 copy.720
  919.8 7.2 add_select_fusion.6
  927.0 6.7 copy.720
  982.4 7.2 add_select_fusion.6
  989.5 6.7 copy.720
  1044.9 7.2 add_select_fusion.6
  1052.1 6.7 copy.720
  1107.5 7.2 add_select_fusion.6
  1114.7 6.7 copy.720
  1170.1 7.2 add_select_fusion.6
  1177.3 6.7 copy.720
  1232.8 7.2 add_select_fusion.6
  1239.9 6.7 copy.720
  1295.4 7.2 add_select_fusion.6
  1302.6 6.7 copy.720
  1358.0 7.2 add_select_fusion.6
  1420.6 7.2 add_select_fusion.6
  1483.2 7.2 add_select_fusion.6
  1504.8 8.2 gather_fusion.3
  1518.4 11.3 select_reduce_fusion
  1539.1 11.1 all-reduce.12.cloned.1.call-done
  1670.6 7.0 collective-permute-start.45
  1677.5 7.8 collective-permute-start.60
  1685.3 7.8 collective-permute-start.46
  1693.1 7.7 collective-permute-start.61
  1700.8 8.2 collective-permute-start.47
  1741.0 7.9 collective-permute-start.62
  1748.9 7.0 collective-permute-start.48
  1755.9 7.0 collective-permute-start.63
  1779.2 71.9 %collective-permute-done.49 = bf16[512,6,64]{0,2,1:T(8,128)(2,1)S(1)} collective-permute-done((bf16[512,6,64]{0,2,1:T(8,128)(2,1)S(1)}, bf16[512,6,64]{0,2,1:T(8,128)(2,1)S(1)}, u32[]{:S(2)}, u32[]{:S(2)}) %collective-permute-start.49) | collective-permute-done | bytes 393248 | tf_op jit(solution)/shard_map/ppermute | solution.py:25
  1869.3 7.6 collective-permute-done.65
  1877.6 7.7 collective-permute-done.51
  1886.0 41.5 %collective-permute-done.66 = bf16[512,6,64]{0,2,1:T(8,128)(2,1)S(1)} collective-permute-done((bf16[512,6,64]{0,2,1:T(8,128)(2,1)S(1)}, bf16[512,6,64]{0,2,1:T(8,128)(2,1)S(1)}, u32[]{:S(2)}, u32[]{:S(2)}) %collective-permute-start.66) | collective-permute-done | bytes 393248 | tf_op jit(solution)/shard_map/ppermute | solution.py:25
  1928.2 7.7 collective-permute-done.52
  1938.3 14.8 collective-permute-done.67
  1997.6 124.4 %reduce-scatter.19.cloned.1.call-done = f32[48,8]{1,0:T(8,128)} async-done(((f32[768,8]{1,0:T(8,128)}), f32[48,8]{1,0:T(8,128)}) %reduce-scatter.19.cloned.1.call-update) | async-done | bytes 1552
  2123.4 24.5 all-reduce.16.cloned.1.call-done
  2149.8 28.5 all-reduce.3
  2184.3 149.5 %all-reduce.14.cloned.1.call-done = f32[3,768,384]{2,0,1:T(4,128)} async-done(((f32[3,768,384]{2,0,1:T(4,128)}), f32[3,768,384]{2,0,1:T(4,128)}) %all-reduce.14.cloned.1.call-update) | async-done | bytes 3538960
  2335.5 125.3 %reduce-scatter.13.cloned.1.call-done = f32[384,48]{0,1:T(8,128)} async-done(((f32[384,768]{0,1:T(8,128)}), f32[384,48]{0,1:T(8,128)}) %reduce-scatter.13.cloned.1.call-update) | async-done | bytes 73744 | tf_op jit(solution)/shard_map/reduce_scatter | solution.py:411
  2460.8 212.3 %reduce-scatter.17.cloned.1.call-done = f32[4,1024,48]{1,2,0:T(8,128)} async-done(((f32[4,1024,768]{1,2,0:T(8,128)}), f32[4,1024,48]{1,2,0:T(8,128)}) %reduce-scatter.17.cloned.1.call-update) | async-done | bytes 786448 | tf_op jit(solution)/shard_map/reduce_scatter | solution.py:417
  2673.2 367.4 %reduce-scatter.15.cloned.1.call-done = f32[4,2,48,1024]{3,2,1,0:T(8,128)} async-done(((f32[4,2,768,1024]{3,2,1,0:T(8,128)}), f32[4,2,48,1024]{3,2,1,0:T(8,128)}) %reduce-scatter.15.cloned.1.call-update) | async-done | bytes 1572880 | tf_op jit(solution)/shard_map/reduce_scatter | solution.py:416
  (1247 shorter events, 1243.5 us)
Async XLA Ops:
  7.2 537.2 %all-reduce.10.cloned.1.call-start = ((), (), s32[]{:S(2)}) async-start(), calls=%async_computation.6 | async-start | bytes 1572864 | tf_op jit(solution)/shard_map/psum | solution.py:156
  7.2 40.6 %collective-permute-start.24 = (s32[512]{0:T(512)}, s32[512]{0:T(512)S(1)}, u32[]{:S(2)}, u32[]{:S(2)}) collective-permute-start(s32[512]{0:T(512)} %param.23), channel_id=1, source_target_pairs={{0,26},{2,28},{4,30},{1,27},{3,29},{5,31}} | collective-permute-start | bytes 6152 | tf_op jit(solution)/shard_map/ppermute | solution.py:25
  8.0 45.5 %collective-permute-start.22 = (s32[512]{0:T(512)}, s32[512]{0:T(512)S(1)}, u32[]{:S(2)}, u32[]{:S(2)}) collective-permute-start(s32[512]{0:T(512)} %param.23), channel_id=1, source_target_pairs={{0,24},{2,26},{4,28},{6,30},{1,25},{3,27},{5,29},{7,31}} | collective-permute-start | bytes 6152 | tf_op jit(solution)/shard_map/ppermute | solution.py:25
  8.7 46.8 %collective-permute-start.2 = (s32[512]{0:T(512)}, s32[512]{0:T(512)S(1)}, u32[]{:S(2)}, u32[]{:S(2)}) collective-permute-start(s32[512]{0:T(512)} %param.23), channel_id=1, source_target_pairs={{0,4},{2,6},{4,8},{6,10},{8,12},{10,14},{12,16},{14,18},{16,20},{1... | collective-permute-start | bytes 6152 | tf_op jit(solution)/shard_map/ppermute | solution.py:25
  11.9 45.6 %collective-permute-start.28 = (s32[512]{0:T(512)}, s32[512]{0:T(512)S(1)}, u32[]{:S(2)}, u32[]{:S(2)}) collective-permute-start(s32[512]{0:T(512)} %param.23), channel_id=1, source_target_pairs={{0,30},{1,31}} | collective-permute-start | bytes 6152 | tf_op jit(solution)/shard_map/ppermute | solution.py:25
  12.5 47.3 %collective-permute-start.26 = (s32[512]{0:T(512)}, s32[512]{0:T(512)S(1)}, u32[]{:S(2)}, u32[]{:S(2)}) collective-permute-start(s32[512]{0:T(512)} %param.23), channel_id=1, source_target_pairs={{0,28},{2,30},{1,29},{3,31}} | collective-permute-start | bytes 6152 | tf_op jit(solution)/shard_map/ppermute | solution.py:25
  47.8 15.6 collective-permute-start.12
  53.6 10.5 collective-permute-start.10
  55.5 9.3 collective-permute-start.8
  70.6 186.0 %collective-permute-start.27 = (bf16[512,6,64]{0,2,1:T(8,128)(2,1)}, bf16[512,6,64]{0,2,1:T(8,128)(2,1)S(1)}, u32[]{:S(2)}, u32[]{:S(2)}) collective-permute-start(bf16[512,6,64]{0,2,1:T(8,128)(2,1)} %pad_maximum_fusion.7), channel_id=1, source_target_pairs={{0,28},{2,30},{1,29},{3,31}} | collective-permute-start | bytes 1179656 | tf_op jit(solution)/shard_map/ppermute | solution.py:25
  71.3 180.0 %collective-permute-start.25 = (bf16[512,6,64]{0,2,1:T(8,128)(2,1)}, bf16[512,6,64]{0,2,1:T(8,128)(2,1)S(1)}, u32[]{:S(2)}, u32[]{:S(2)}) collective-permute-start(bf16[512,6,64]{0,2,1:T(8,128)(2,1)} %pad_maximum_fusion.7), channel_id=1, source_target_pairs={{0,26},{2,28},{4,30},{1,27},{3,29},{5,31}} | collective-permute-start | bytes 1179656 | tf_op jit(solution)/shard_map/ppermute | solution.py:25
  72.0 173.8 %collective-permute-start.23 = (bf16[512,6,64]{0,2,1:T(8,128)(2,1)}, bf16[512,6,64]{0,2,1:T(8,128)(2,1)S(1)}, u32[]{:S(2)}, u32[]{:S(2)}) collective-permute-start(bf16[512,6,64]{0,2,1:T(8,128)(2,1)} %pad_maximum_fusion.7), channel_id=1, source_target_pairs={{0,24},{2,26},{4,28},{6,30},{1,25},{3,27},{5,29},{7,31}} | collective-permute-start | bytes 1179656 | tf_op jit(solution)/shard_map/ppermute | solution.py:25
  73.4 167.1 %collective-permute-start.21 = (bf16[512,6,64]{0,2,1:T(8,128)(2,1)}, bf16[512,6,64]{0,2,1:T(8,128)(2,1)S(1)}, u32[]{:S(2)}, u32[]{:S(2)}) collective-permute-start(bf16[512,6,64]{0,2,1:T(8,128)(2,1)} %pad_maximum_fusion.7), channel_id=1, source_target_pairs={{0,22},{2,24},{4,26},{6,28},{8,30},{1,23},{3,25},{5,27},{7,29},{9,... | collective-permute-start | bytes 1179656 | tf_op jit(solution)/shard_map/ppermute | solution.py:25
  81.2 24.7 collective-permute-start.1
  105.9 13.2 collective-permute-start.3
  119.1 14.0 collective-permute-start.5
  133.1 22.4 collective-permute-start.7
  155.5 11.5 collective-permute-start.9
  167.0 11.5 collective-permute-start.11
  178.5 19.8 collective-permute-start.13
  198.3 28.6 collective-permute-start.15
  235.3 201.6 %collective-permute-start.44 = (bf16[512,6,64]{0,2,1:T(8,128)(2,1)S(1)}, bf16[512,6,64]{0,2,1:T(8,128)(2,1)S(1)}, u32[]{:S(2)}, u32[]{:S(2)}) collective-permute-start(bf16[512,6,64]{0,2,1:T(8,128)(2,1)S(1)} %bitcast.506), channel_id=1, source_target_pairs={{0,30},{1,31}} | collective-permute-start | bytes 1179656 | tf_op jit(solution)/shard_map/ppermute | solution.py:25
  240.5 194.3 %collective-permute-start.43 = (bf16[512,6,64]{0,2,1:T(8,128)(2,1)S(1)}, bf16[512,6,64]{0,2,1:T(8,128)(2,1)S(1)}, u32[]{:S(2)}, u32[]{:S(2)}) collective-permute-start(bf16[512,6,64]{0,2,1:T(8,128)(2,1)S(1)} %bitcast.507), channel_id=1, source_target_pairs={{0,28},{2,30},{1,29},{3,31}} | collective-permute-start | bytes 1179656 | tf_op jit(solution)/shard_map/ppermute | solution.py:25
  245.8 186.1 %collective-permute-start.42 = (bf16[512,6,64]{0,2,1:T(8,128)(2,1)S(1)}, bf16[512,6,64]{0,2,1:T(8,128)(2,1)S(1)}, u32[]{:S(2)}, u32[]{:S(2)}) collective-permute-start(bf16[512,6,64]{0,2,1:T(8,128)(2,1)S(1)} %bitcast.508), channel_id=1, source_target_pairs={{0,26},{2,28},{4,30},{1,27},{3,29},{5,31}} | collective-permute-start | bytes 1179656 | tf_op jit(solution)/shard_map/ppermute | solution.py:25
  251.3 177.8 %collective-permute-start.41 = (bf16[512,6,64]{0,2,1:T(8,128)(2,1)S(1)}, bf16[512,6,64]{0,2,1:T(8,128)(2,1)S(1)}, u32[]{:S(2)}, u32[]{:S(2)}) collective-permute-start(bf16[512,6,64]{0,2,1:T(8,128)(2,1)S(1)} %bitcast.509), channel_id=1, source_target_pairs={{0,24},{2,26},{4,28},{6,30},{1,25},{3,27},{5,29},{7,31}} | collective-permute-start | bytes 1179656 | tf_op jit(solution)/shard_map/ppermute | solution.py:25
  256.6 37.0 %collective-permute-start.31 = (bf16[512,6,64]{0,2,1:T(8,128)(2,1)S(1)}, bf16[512,6,64]{0,2,1:T(8,128)(2,1)S(1)}, u32[]{:S(2)}, u32[]{:S(2)}) collective-permute-start(bf16[512,6,64]{0,2,1:T(8,128)(2,1)S(1)} %bitcast.510), channel_id=1, source_target_pairs={{0,4},{2,6},{4,8},{6,10},{8,12},{10,14},{12,16},{14,18},{16,20},{1... | collective-permute-start | bytes 1179656 | tf_op jit(solution)/shard_map/ppermute | solution.py:25
  293.6 28.0 collective-permute-start.32
  321.6 15.9 collective-permute-start.33
  337.6 11.3 collective-permute-start.34
  348.9 10.9 collective-permute-start.35
  359.8 26.2 collective-permute-start.36
  386.0 20.2 collective-permute-start.37
  416.9 22.3 collective-permute-start.30
  446.7 1103.6 %all-reduce.12.cloned.1.call-start = ((), (), s32[]{:S(2)}) async-start(), calls=%async_computation.7 | async-start | bytes 1572864 | tf_op jit(solution)/shard_map/psum | solution.py:284
  1529.7 465.1 %reduce-scatter.23.cloned.1.call-start = ((), (), s32[]{:S(2)}) async-start(), calls=%async_computation.13 | async-start | bytes 417792
  1536.6 459.6 %reduce-scatter.21.cloned.1.call-start = ((), (), s32[]{:S(2)}) async-start(), calls=%async_computation.12 | async-start | bytes 417792
  1538.4 583.7 %reduce-scatter.19.cloned.1.call-start = ((), (), s32[]{:S(2)}) async-start(), calls=%async_computation.11 | async-start | bytes 417792
  1539.1 608.9 %all-reduce.16.cloned.1.call-start = ((), (), s32[]{:S(2)}) async-start(), calls=%async_computation.15 | async-start | bytes 3145728 | tf_op jit(solution)/shard_map/psum | solution.py:226
  1670.6 70.4 %collective-permute-start.45 = (bf16[512,6,64]{0,2,1:T(8,128)(2,1)}, bf16[512,6,64]{0,2,1:T(8,128)(2,1)}, u32[]{:S(2)}, u32[]{:S(2)}) collective-permute-start(bf16[512,6,64]{0,2,1:T(8,128)(2,1)} %fusion.304), channel_id=1, source_target_pairs={{2,0},{4,2},{6,4},{8,6},{10,8},{12,10},{14,12},{16,14},{18,16},{20... | collective-permute-start | bytes 1179656 | tf_op jit(solution)/shard_map/ppermute | solution.py:25
  1677.5 71.3 %collective-permute-start.60 = (bf16[512,6,64]{0,2,1:T(8,128)(2,1)}, bf16[512,6,64]{0,2,1:T(8,128)(2,1)}, u32[]{:S(2)}, u32[]{:S(2)}) collective-permute-start(bf16[512,6,64]{0,2,1:T(8,128)(2,1)} %fusion.347), channel_id=1, source_target_pairs={{2,0},{4,2},{6,4},{8,6},{10,8},{12,10},{14,12},{16,14},{18,16},{20... | collective-permute-start | bytes 1179656 | tf_op jit(solution)/shard_map/ppermute | solution.py:25
  1685.3 70.6 %collective-permute-start.46 = (bf16[512,6,64]{0,2,1:T(8,128)(2,1)}, bf16[512,6,64]{0,2,1:T(8,128)(2,1)}, u32[]{:S(2)}, u32[]{:S(2)}) collective-permute-start(bf16[512,6,64]{0,2,1:T(8,128)(2,1)} %fusion.303), channel_id=1, source_target_pairs={{4,0},{6,2},{8,4},{10,6},{12,8},{14,10},{16,12},{18,14},{20,16},{2... | collective-permute-start | bytes 1179656 | tf_op jit(solution)/shard_map/ppermute | solution.py:25
  1693.1 69.9 %collective-permute-start.61 = (bf16[512,6,64]{0,2,1:T(8,128)(2,1)}, bf16[512,6,64]{0,2,1:T(8,128)(2,1)}, u32[]{:S(2)}, u32[]{:S(2)}) collective-permute-start(bf16[512,6,64]{0,2,1:T(8,128)(2,1)} %fusion.344), channel_id=1, source_target_pairs={{4,0},{6,2},{8,4},{10,6},{12,8},{14,10},{16,12},{18,14},{20,16},{2... | collective-permute-start | bytes 1179656 | tf_op jit(solution)/shard_map/ppermute | solution.py:25
  1700.8 65.5 %collective-permute-start.47 = (bf16[512,6,64]{0,2,1:T(8,128)(2,1)}, bf16[512,6,64]{0,2,1:T(8,128)(2,1)}, u32[]{:S(2)}, u32[]{:S(2)}) collective-permute-start(bf16[512,6,64]{0,2,1:T(8,128)(2,1)} %fusion.302), channel_id=1, source_target_pairs={{6,0},{8,2},{10,4},{12,6},{14,8},{16,10},{18,12},{20,14},{22,16},{... | collective-permute-start | bytes 1179656 | tf_op jit(solution)/shard_map/ppermute | solution.py:25
  1741.0 29.1 collective-permute-start.62
  1748.9 23.3 collective-permute-start.48
  1755.9 20.2 collective-permute-start.63
  1763.0 88.1 %collective-permute-start.49 = (bf16[512,6,64]{0,2,1:T(8,128)(2,1)S(1)}, bf16[512,6,64]{0,2,1:T(8,128)(2,1)S(1)}, u32[]{:S(2)}, u32[]{:S(2)}) collective-permute-start(bf16[512,6,64]{0,2,1:T(8,128)(2,1)S(1)} %copy-done.85), channel_id=1, source_target_pairs={{10,0},{12,2},{14,4},{16,6},{18,8},{20,10},{22,12},{24,14},{26,16}... | collective-permute-start | bytes 1179656 | tf_op jit(solution)/shard_map/ppermute | solution.py:25
  1766.3 93.2 %collective-permute-start.64 = (bf16[512,6,64]{0,2,1:T(8,128)(2,1)S(1)}, bf16[512,6,64]{0,2,1:T(8,128)(2,1)S(1)}, u32[]{:S(2)}, u32[]{:S(2)}) collective-permute-start(bf16[512,6,64]{0,2,1:T(8,128)(2,1)S(1)} %copy-done.207), channel_id=1, source_target_pairs={{10,0},{12,2},{14,4},{16,6},{18,8},{20,10},{22,12},{24,14},{26,16}... | collective-permute-start | bytes 1179656 | tf_op jit(solution)/shard_map/ppermute | solution.py:25
  1770.1 97.9 %collective-permute-start.50 = (bf16[512,6,64]{0,2,1:T(8,128)(2,1)S(1)}, bf16[512,6,64]{0,2,1:T(8,128)(2,1)S(1)}, u32[]{:S(2)}, u32[]{:S(2)}) collective-permute-start(bf16[512,6,64]{0,2,1:T(8,128)(2,1)S(1)} %fusion.299), channel_id=1, source_target_pairs={{12,0},{14,2},{16,4},{18,6},{20,8},{22,10},{24,12},{26,14},{28,16}... | collective-permute-start | bytes 1179656 | tf_op jit(solution)/shard_map/ppermute | solution.py:25
  1772.1 104.8 %collective-permute-start.65 = (bf16[512,6,64]{0,2,1:T(8,128)(2,1)S(1)}, bf16[512,6,64]{0,2,1:T(8,128)(2,1)S(1)}, u32[]{:S(2)}, u32[]{:S(2)}) collective-permute-start(bf16[512,6,64]{0,2,1:T(8,128)(2,1)S(1)} %copy-done.206), channel_id=1, source_target_pairs={{12,0},{14,2},{16,4},{18,6},{20,8},{22,10},{24,12},{26,14},{28,16}... | collective-permute-start | bytes 1179656 | tf_op jit(solution)/shard_map/ppermute | solution.py:25
  1776.1 109.1 %collective-permute-start.51 = (bf16[512,6,64]{0,2,1:T(8,128)(2,1)S(1)}, bf16[512,6,64]{0,2,1:T(8,128)(2,1)S(1)}, u32[]{:S(2)}, u32[]{:S(2)}) collective-permute-start(bf16[512,6,64]{0,2,1:T(8,128)(2,1)S(1)} %copy-done.84), channel_id=1, source_target_pairs={{14,0},{16,2},{18,4},{20,6},{22,8},{24,10},{26,12},{28,14},{30,16}... | collective-permute-start | bytes 1179656 | tf_op jit(solution)/shard_map/ppermute | solution.py:25
  1851.1 76.4 %collective-permute-start.66 = (bf16[512,6,64]{0,2,1:T(8,128)(2,1)S(1)}, bf16[512,6,64]{0,2,1:T(8,128)(2,1)S(1)}, u32[]{:S(2)}, u32[]{:S(2)}) collective-permute-start(bf16[512,6,64]{0,2,1:T(8,128)(2,1)S(1)} %copy-done.205), channel_id=1, source_target_pairs={{14,0},{16,2},{18,4},{20,6},{22,8},{24,10},{26,12},{28,14},{30,16}... | collective-permute-start | bytes 1179656 | tf_op jit(solution)/shard_map/ppermute | solution.py:25
  1859.5 76.4 %collective-permute-start.52 = (bf16[512,6,64]{0,2,1:T(8,128)(2,1)S(1)}, bf16[512,6,64]{0,2,1:T(8,128)(2,1)S(1)}, u32[]{:S(2)}, u32[]{:S(2)}) collective-permute-start(bf16[512,6,64]{0,2,1:T(8,128)(2,1)S(1)} %copy-done.83), channel_id=1, source_target_pairs={{16,0},{18,2},{20,4},{22,6},{24,8},{26,10},{28,12},{30,14},{17,1},... | collective-permute-start | bytes 1179656 | tf_op jit(solution)/shard_map/ppermute | solution.py:25
  1867.9 85.2 %collective-permute-start.67 = (bf16[512,6,64]{0,2,1:T(8,128)(2,1)S(1)}, bf16[512,6,64]{0,2,1:T(8,128)(2,1)S(1)}, u32[]{:S(2)}, u32[]{:S(2)}) collective-permute-start(bf16[512,6,64]{0,2,1:T(8,128)(2,1)S(1)} %copy-done.204), channel_id=1, source_target_pairs={{16,0},{18,2},{20,4},{22,6},{24,8},{26,10},{28,12},{30,14},{17,1},... | collective-permute-start | bytes 1179656 | tf_op jit(solution)/shard_map/ppermute | solution.py:25
  1876.9 77.0 %collective-permute-start.53 = (bf16[512,6,64]{0,2,1:T(8,128)(2,1)S(1)}, bf16[512,6,64]{0,2,1:T(8,128)(2,1)S(1)}, u32[]{:S(2)}, u32[]{:S(2)}) collective-permute-start(bf16[512,6,64]{0,2,1:T(8,128)(2,1)S(1)} %fusion.296), channel_id=1, source_target_pairs={{18,0},{20,2},{22,4},{24,6},{26,8},{28,10},{30,12},{19,1},{21,3},{... | collective-permute-start | bytes 1179656 | tf_op jit(solution)/shard_map/ppermute | solution.py:25
  1885.3 69.3 %collective-permute-start.68 = (bf16[512,6,64]{0,2,1:T(8,128)(2,1)S(1)}, bf16[512,6,64]{0,2,1:T(8,128)(2,1)S(1)}, u32[]{:S(2)}, u32[]{:S(2)}) collective-permute-start(bf16[512,6,64]{0,2,1:T(8,128)(2,1)S(1)} %copy-done.203), channel_id=1, source_target_pairs={{18,0},{20,2},{22,4},{24,6},{26,8},{28,10},{30,12},{19,1},{21,3},{... | collective-permute-start | bytes 1179656 | tf_op jit(solution)/shard_map/ppermute | solution.py:25
  1927.5 27.8 collective-permute-start.54
  1935.9 20.1 collective-permute-start.69
  1957.9 11.2 collective-permute-start.70
  1959.4 9.7 collective-permute-start.71
  1978.3 355.5 %all-reduce.14.cloned.1.call-start = ((), (), s32[]{:S(2)}) async-start(), calls=%async_computation.14 | async-start | bytes 9437184
  1988.9 471.9 %reduce-scatter.13.cloned.1.call-start = ((), (), s32[]{:S(2)}) async-start(), calls=%async_computation.8 | async-start | bytes 1253376 | tf_op jit(solution)/shard_map/reduce_scatter | solution.py:411
  1992.1 681.1 %reduce-scatter.17.cloned.1.call-start = ((), (), s32[]{:S(2)}) async-start(), calls=%async_computation.10 | async-start | bytes 13369344 | tf_op jit(solution)/shard_map/reduce_scatter | solution.py:417
  1992.9 1047.7 %reduce-scatter.15.cloned.1.call-start = ((), (), s32[]{:S(2)}) async-start(), calls=%async_computation.9 | async-start | bytes 26738688 | tf_op jit(solution)/shard_map/reduce_scatter | solution.py:416
  (316 other events, 13288.5 us)
Sparse Core Ops, SparseCore 0:
  446.8 97.5 all-reduce.9
  1529.8 20.3 all-reduce.11
  1554.9 119.5 reduce-scatter.22
  1679.7 197.8 reduce-scatter.20
  1882.1 239.9 reduce-scatter.18
  2125.0 22.9 all-reduce.15
  2153.7 180.1 all-reduce.13
  2339.9 120.9 reduce-scatter.12
  2468.0 205.1 reduce-scatter.16
  2679.3 361.1 reduce-scatter.14
where the time goes:
time: 3070 us; the launch traced here: 3050 us
  waiting for transfers between devices  1420 us (46%)
  local copies, waits for them, and re-layouts  620 us (20%)
  matrix products  582 us (19%)
  starting transfers between devices  231 us (8%)
  other arithmetic  93.2 us (3%)
  loops' own time  47.5 us (2%)
  blocking collectives  31 us (1%)
    reduce_scatter x1, waiting for transfers between devices, local(): lax.psum_scatter(w_gu_local, 'dp', scatter_dimension=2, tiled=True)  367 us
    ppermute x75, waiting for transfers between devices, passed_along(): return lax.ppermute(block, axis, route)  316 us
    unnamed x14, waiting for transfers between devices  275 us
    another operation x51, local copies, waits for them, and re-layouts  254 us
    ppermute x75, starting transfers between devices, passed_along(): return lax.ppermute(block, axis, route)  230 us
    reduce_scatter x1, waiting for transfers between devices, local(): lax.psum_scatter(w_down_local, 'dp', scatter_dimension=2, tiled=True)  212 us
    reduce_scatter x1, waiting for transfers between devices, local(): lax.psum_scatter(out_grad_local, 'dp', scatter_dimension=1, tiled=True)  125 us
    scatter-add x24, local copies, waits for them, and re-layouts, grad_scan(): gu_total = gu_total.at[operand[4]].add(gu_step)  119 us
  transfers between devices with their start and end apart: 85, of which 33 were waited for; matrix products, arithmetic and copies ran while one was open for 11% of the time, Pallas kernels for 0%

commit v1 on v0

v1 whole, which is shorter than its diff:
```python
import functools
import math

import jax
import jax.numpy as jnp
import numpy as np
from jax import lax
from jax.experimental import pallas as pl
from jax.experimental.pallas import tpu as pltpu
from jax.sharding import Mesh
from jax.sharding import PartitionSpec as P

f32 = jnp.float32
bf = jnp.bfloat16
E_FFN = 4
NCONST = 2
E_ALL = 8
SPAN = 16
SEQ_LEN = 8192
EPSILON = 1e-05
HIGHEST = lax.Precision.HIGHEST
GROUP = ("z", "y", "x")
GATE_ROWS = 16


HD = 64
NEG = -1e30
WIDE = (4, 2, 1)


def dotf(a, b, ca, cb):
    return lax.dot_general(a, b, (((ca,), (cb,)), ((), ())), preferred_element_type=f32)


def key_places(t, blocks, half):
    r = lax.broadcasted_iota(jnp.int32, (blocks * 2 * half, half), 0)
    inside = r % (2 * half)
    return r - inside + jnp.where(inside < half, t * half + inside, (1 - t) * half + inside - half)


def fwd_kernel(nb, half, sc, start_ref, own_ref, oth_ref, o_ref, of_ref, lse_ref, ktm, vt):
    keys = 2 * half
    t = sc[0]

    def prep(j, _):
        at = pl.ds(pl.multiple_of(j * keys, keys), half)
        more = pl.ds(pl.multiple_of(j * keys + half, half), half)
        ktm[at, :] = own_ref[j, HD : 2 * HD, :].T
        ktm[more, :] = oth_ref[j, 0:HD, :].T
        vt[:, at] = own_ref[j, 2 * HD : 3 * HD, :]
        vt[:, more] = oth_ref[j, HD : 2 * HD, :]
        return 0

    lax.fori_loop(0, nb, prep, 0)
    lane = lax.broadcasted_iota(jnp.int32, (1, half), 1)

    def qblock(s, _):
        q = own_ref[s, 0:HD, :] * bf(0.125)
        start_row = start_ref[s]
        last_row = s * keys + t * half + lane
        lo, ml = sc[1 + s], jnp.minimum(sc[1 + nb + s], s)

        def scores(j, n):
            return dotf(ktm[pl.ds(pl.multiple_of(j * keys, keys), n * keys), :], q, 1, 0)

        def allowed(j, n):
            place = key_places(t, n, half) + j * keys
            return (place >= start_row) & (place <= last_row)

        def values(j, n):
            return vt[:, pl.ds(pl.multiple_of(j * keys, keys), n * keys)]

        def emit(o, lse):
            o_ref[s] = o.astype(bf)
            of_ref[s] = o
            lse_ref[s] = lse

        def plain(j, n, c, masked):
            l, acc = c
            p = jnp.exp(scores(j, n))
            if masked:
                p = jnp.where(allowed(j, n), p, 0.0)
            return l + jnp.sum(p, axis=0, keepdims=True), acc + dotf(values(j, n), p.astype(bf), 1, 0)

        c = (jnp.zeros((1, half), f32), jnp.zeros((HD, half), f32))
        c = plain(s, 1, c, True)
        for masked, first, end in ((True, lo, ml), (False, jnp.maximum(lo, ml), s)):
            for n in WIDE:
                count = jnp.maximum(end - first, 0) // n
                c = lax.fori_loop(0, count, lambda i, c: plain(first + i * n, n, c, masked), c)
                first = first + count * n
        l, acc = c
        emit(acc / l, jnp.log(l))
        fine = (jnp.min(l) > 1e-25) & (jnp.max(l) < 1e25)

        @pl.when(jnp.logical_not(fine))
        def _():
            def shifted(j, c):
                m, l, acc = c
                sco = jnp.where(allowed(j, 1), scores(j, 1), NEG)
                mn = jnp.maximum(m, jnp.max(sco, axis=0, keepdims=True))
                p = jnp.exp(sco - mn)
                al = jnp.exp(m - mn)
                return mn, l * al + jnp.sum(p, axis=0, keepdims=True), acc * al + dotf(values(j, 1), p.astype(bf), 1, 0)

            c = (jnp.full((1, half), NEG, f32), jnp.zeros((1, half), f32), jnp.zeros((HD, half), f32))
            c = shifted(s, c)
            m, l, acc = lax.fori_loop(lo, s, shifted, c)
            emit(acc / l, m + jnp.log(l))

        return 0

    lax.fori_loop(0, nb, qblock, 0)


def flash_fwd(sc, start, own, oth):
    nb, _, half = own.shape
    v = pl.BlockSpec(memory_space=pltpu.VMEM)
    return pl.pallas_call(
        functools.partial(fwd_kernel, nb, half),
        out_shape=(
            jax.ShapeDtypeStruct((nb, HD, half), bf),
            jax.ShapeDtypeStruct((nb, HD, half), f32),
            jax.ShapeDtypeStruct((nb, 1, half), f32),
        ),
        in_specs=[pl.BlockSpec(memory_space=pltpu.SMEM), v, v, v],
        out_specs=(v, v, v),
        scratch_shapes=[pltpu.VMEM((nb * 2 * half, HD), bf), pltpu.VMEM((HD, nb * 2 * half), bf)],
        compiler_params=pltpu.CompilerParams(vmem_limit_bytes=48 << 20),
        cost_estimate=pl.CostEstimate(flops=10**9, bytes_accessed=4 << 20, transcendentals=10**6),
        name="flash_fwd",
    )(sc, start, own, oth)


def bwd_kernel(
    nb, half, j0, j1, sc, start_ref, own_ref, oth_ref, do_ref, of_ref, lse_ref,
    dq_ref, dko_ref, dkx_ref, ktm, vtm, kt, qt, dot, dq_acc, dotm, qtm, stats,
):
    keys = 2 * half
    t = sc[0]

    def prep(j, _):
        k = j - j0
        ktm[k, 0:half, :] = own_ref[j, HD : 2 * HD, :].T
        ktm[k, half:keys, :] = oth_ref[j, 0:HD, :].T
        vtm[k, 0:half, :] = own_ref[j, 2 * HD : 3 * HD, :].T
        vtm[k, half:keys, :] = oth_ref[j, HD : 2 * HD, :].T
        kt[k, :, 0:half] = own_ref[j, HD : 2 * HD, :]
        kt[k, :, half:keys] = oth_ref[j, 0:HD, :]
        return 0

    lax.fori_loop(j0, j1, prep, 0)

    def prep_q(s, _):
        at = pl.ds(pl.multiple_of(s * half, half), half)
        q = own_ref[s, 0:HD, :] * bf(0.125)
        qt[:, at] = q
        qtm[at, :] = q.T
        dot[:, at] = do_ref[s]
        dotm[at, :] = do_ref[s].T
        dq_acc[:, at] = jnp.zeros((HD, half), f32)
        stats[0:1, at] = lse_ref[s]
        stats[1:2, at] = jnp.sum(do_ref[s].astype(f32) * of_ref[s], axis=0, keepdims=True)
        return 0

    lax.fori_loop(j0, nb, prep_q, 0)
    lane = lax.broadcasted_iota(jnp.int32, (1, half), 1)

    def kblock(j, _):
        k = j - j0
        kj, vj, ktj = ktm[k], vtm[k], kt[k]

        def tile(s, n, c, masked):
            dk, dv = c
            at = pl.ds(pl.multiple_of(s * half, half), n * half)
            sco = dotf(kj, qt[:, at], 1, 0)
            if masked:
                place = key_places(t, 1, half) + j * keys
                last_row = s * keys + t * half + lane
                sco = jnp.where((place >= start_ref[s]) & (place <= last_row), sco, NEG)
            p = jnp.exp(sco - stats[0:1, at])
            dp = dotf(vj, dot[:, at], 1, 0)
            ds = (p * (dp - stats[1:2, at])).astype(bf)
            dv = dv + dotf(p.astype(bf), dotm[at, :], 1, 0)
            dk = dk + dotf(ds, qtm[at, :], 1, 0)
            dq_acc[:, at] += dotf(ktj, ds, 1, 0)
            return dk, dv

        c = (jnp.zeros((keys, HD), f32), jnp.zeros((keys, HD), f32))
        c = tile(j, 1, c, True)
        mid, hi = sc[1 + 2 * nb + j], sc[1 + 3 * nb + j]
        first = j + 1
        for n in WIDE:
            count = jnp.maximum(mid - first, 0) // n
            c = lax.fori_loop(0, count, lambda i, c: tile(first + i * n, n, c, False), c)
            first = first + count * n
        dk, dv = lax.fori_loop(jnp.maximum(j + 1, mid), hi, lambda s, c: tile(s, 1, c, True), c)
        dk = dk.T
        dv = dv.T
        dko_ref[k, 0:HD, :] = dk[:, 0:half]
        dko_ref[k, HD : 2 * HD, :] = dv[:, 0:half]
        dkx_ref[k, 0:HD, :] = dk[:, half:keys].astype(bf)
        dkx_ref[k, HD : 2 * HD, :] = dv[:, half:keys].astype(bf)
        return 0

    lax.fori_loop(j0, j1, kblock, 0)

    def finish(s, _):
        at = pl.ds(pl.multiple_of(s * half, half), half)
        dq_ref[s] = (dq_acc[:, at] * 0.125).astype(bf)
        return 0

    def nothing(s, _):
        dq_ref[s] = jnp.zeros((HD, half), bf)
        return 0

    lax.fori_loop(0, j0, nothing, 0)
    lax.fori_loop(j0, nb, finish, 0)


def flash_bwd(sc, start, own, oth, do, of, lse, j0, j1):
    nb, _, half = own.shape
    v = pl.BlockSpec(memory_space=pltpu.VMEM)
    n = j1 - j0
    return pl.pallas_call(
        functools.partial(bwd_kernel, nb, half, j0, j1),
        out_shape=(
            jax.ShapeDtypeStruct((nb, HD, half), bf),
            jax.ShapeDtypeStruct((n, 2 * HD, half), f32),
            jax.ShapeDtypeStruct((n, 2 * HD, half), bf),
        ),
        in_specs=[pl.BlockSpec(memory_space=pltpu.SMEM)] + [v] * 6,
        out_specs=(v, v, v),
        scratch_shapes=[
            pltpu.VMEM((n, 2 * half, HD), bf),
            pltpu.VMEM((n, 2 * half, HD), bf),
            pltpu.VMEM((n, HD, 2 * half), bf),
            pltpu.VMEM((HD, nb * half), bf),
            pltpu.VMEM((HD, nb * half), bf),
            pltpu.VMEM((HD, nb * half), f32),
            pltpu.VMEM((nb * half, HD), bf),
            pltpu.VMEM((nb * half, HD), bf),
            pltpu.VMEM((8, nb * half), f32),
        ],
        compiler_params=pltpu.CompilerParams(vmem_limit_bytes=56 << 20),
        cost_estimate=pl.CostEstimate(flops=10**9, bytes_accessed=4 << 20, transcendentals=10**6),
        name="flash_bwd",
    )(sc, start, own, oth, do, of, lse)


def bounds(start_all, t, nb, HB):
    st=start_all.reshape(nb,2,HB)
    mine=lax.dynamic_index_in_dim(st,t,1,keepdims=False)
    first=mine[:,0]; last=mine[:,HB-1]
    B=2*HB
    lo=first//B
    ml=(last+B-1)//B
    j=jnp.arange(nb)
    mid=jnp.sum((last[None,:]<=j[:,None]*B).astype(jnp.int32),axis=1)
    hi=jnp.sum((lo[None,:]<=j[:,None]).astype(jnp.int32),axis=1)
    mid=jnp.minimum(mid,hi)
    sc=jnp.concatenate([jnp.full((1,),t,jnp.int32),lo,ml,mid,hi]).astype(jnp.int32)
    return sc,mine[:,None,:]


def ffn_kernel(e_ref, u_ref, wgu_ref, *refs):
    pieces = refs[:8]
    x_out_ref, g_ref, wh_ref, mine_ref, other_ref, held = refs[8:]
    half = u_ref.shape[1]
    width = x_out_ref.shape[2]
    hidden_units = wgu_ref.shape[3]
    e = e_ref[0]
    step = pl.program_id(0)
    for k in range(8):

        @pl.when(step == k)
        def _(k=k):
            held[...] = pieces[k][...]

    gates = held[half : half + GATE_ROWS, 0:half].astype(f32)
    row = lax.broadcasted_iota(jnp.int32, gates.shape, 0)
    gate_row = jnp.sum(jnp.where((row == e) | (row == e + E_FFN), gates, 0.0), axis=0, keepdims=True)
    gate = jnp.broadcast_to(gate_row, (8, half)).T[:, 0:1]
    x = held[0:half, :]
    x_out_ref[0] = x
    chunk = 256
    total = jnp.zeros((half, width), f32)
    dots = jnp.zeros((8, half), f32)
    ones = jnp.ones((8, chunk), bf)
    for first in range(0, hidden_units, chunk):
        cols = slice(first, first + chunk)
        g = dotf(x, wgu_ref[0, 0, :, cols], 1, 0)
        up = dotf(x, wgu_ref[0, 1, :, cols], 1, 0)
        raw = u_ref[0, :, cols].astype(f32)
        sig = jax.nn.sigmoid(g)
        silu = g * sig
        hid = silu * up
        hg = gate * raw
        dgate = (hg * up * (sig + silu * (1.0 - sig))).astype(bf)
        dup = (hg * silu).astype(bf)
        g_ref[0, :, cols] = dgate
        g_ref[0, :, slice(hidden_units + first, hidden_units + first + chunk)] = dup
        wh_ref[0, :, cols] = (gate * hid).astype(bf)
        dots = dots + dotf(ones, (hid * raw).astype(bf), 1, 1)
        total = total + dotf(dgate, wgu_ref[0, 0, :, cols], 1, 1) + dotf(dup, wgu_ref[0, 1, :, cols], 1, 1)
    drow = lax.broadcasted_iota(jnp.int32, (GATE_ROWS, half), 0)
    placed = jnp.where(drow == e, jnp.broadcast_to(dots[0:1, :], (GATE_ROWS, half)), 0.0).astype(bf)

    def put(ref):
        ref[0, 0:half, :] = total.astype(bf)
        ref[0, half : half + GATE_ROWS, :] = jnp.zeros((GATE_ROWS, width), bf)
        ref[0, half : half + GATE_ROWS, 0:half] = placed

    @pl.when(step < 4)
    def _():
        put(mine_ref)

    @pl.when(step >= 4)
    def _():
        put(other_ref)


def expert_pass(e, pieces, raw_all, wgu):
    rows, width = pieces[0].shape
    half = rows - GATE_ROWS
    hidden_units = wgu.shape[3]
    flops = 8 * half * width * hidden_units * 2 * 4
    return pl.pallas_call(
        ffn_kernel,
        out_shape=(
            jax.ShapeDtypeStruct((8, half, width), bf),
            jax.ShapeDtypeStruct((8, half, 2 * hidden_units), bf),
            jax.ShapeDtypeStruct((8, half, hidden_units), bf),
            jax.ShapeDtypeStruct((4, rows, width), bf),
            jax.ShapeDtypeStruct((4, rows, width), bf),
        ),
        grid_spec=pltpu.PrefetchScalarGridSpec(
            num_scalar_prefetch=1,
            grid=(8,),
            in_specs=[
                pl.BlockSpec((1, half, hidden_units), lambda i, e: (i, 0, 0)),
                pl.BlockSpec((1, 2, width, hidden_units), lambda i, e: (e[0], 0, 0, 0)),
            ]
            + [pl.BlockSpec((rows, width), lambda i, e: (0, 0))] * 8,
            out_specs=(
                pl.BlockSpec((1, half, width), lambda i, e: (i, 0, 0)),
                pl.BlockSpec((1, half, 2 * hidden_units), lambda i, e: (i, 0, 0)),
                pl.BlockSpec((1, half, hidden_units), lambda i, e: (i, 0, 0)),
                pl.BlockSpec((1, rows, width), lambda i, e: (jnp.minimum(i, 3), 0, 0)),
                pl.BlockSpec((1, rows, width), lambda i, e: (jnp.maximum(i - 4, 0), 0, 0)),
            ),
            scratch_shapes=[pltpu.VMEM((rows, width), bf)],
        ),
        compiler_params=pltpu.CompilerParams(vmem_limit_bytes=48 << 20),
        cost_estimate=pl.CostEstimate(flops=flops, bytes_accessed=40 << 20, transcendentals=2 << 20),
        name="expert_pass",
    )(e, raw_all, wgu, *pieces)


def hidden_cotangent_kernel(e_ref, w_ref, *refs):
    pieces, up_ref, raw_ref, held = refs[:8], refs[8], refs[9], refs[10]
    for k in range(8):

        @pl.when(pl.program_id(0) == k)
        def _(k=k):
            held[...] = pieces[k][...]

    rows = held[...]
    up_ref[0] = rows
    raw_ref[0] = dotf(rows, w_ref[0], 1, 1).astype(bf)


def hidden_cotangent(e, pieces, w_down):
    half, width = pieces[0].shape
    hidden_units = w_down.shape[1]
    return pl.pallas_call(
        hidden_cotangent_kernel,
        out_shape=(
            jax.ShapeDtypeStruct((8, half, width), bf),
            jax.ShapeDtypeStruct((8, half, hidden_units), bf),
        ),
        grid_spec=pltpu.PrefetchScalarGridSpec(
            num_scalar_prefetch=1,
            grid=(8,),
            in_specs=[pl.BlockSpec((1, hidden_units, width), lambda i, e: (e[0], 0, 0))]
            + [pl.BlockSpec((half, width), lambda i, e: (0, 0))] * 8,
            out_specs=(
                pl.BlockSpec((1, half, width), lambda i, e: (i, 0, 0)),
                pl.BlockSpec((1, half, hidden_units), lambda i, e: (i, 0, 0)),
            ),
            scratch_shapes=[pltpu.VMEM((half, width), bf)],
        ),
        compiler_params=pltpu.CompilerParams(vmem_limit_bytes=40 << 20),
        cost_estimate=pl.CostEstimate(flops=32 * 10**8, bytes_accessed=12 << 20, transcendentals=0),
        name="hidden_cotangent",
    )(e, w_down, *pieces)


def cot_rows_kernel(first_ref, x_ref, own_ref, other_ref, out_ref):
    heads = own_ref.shape[0] // HD
    out_ref[...] = jnp.zeros(out_ref.shape, bf)
    x = x_ref[...]
    for n, ref in enumerate((own_ref, other_ref)):
        rows = dotf(ref[...], x, 1, 1).astype(bf)
        for h in range(heads):
            out_ref[first_ref[n] + h] = rows[h * HD : (h + 1) * HD]


def cot_rows(first, x, own, other):
    v = pl.BlockSpec(memory_space=pltpu.VMEM)
    return pl.pallas_call(
        cot_rows_kernel,
        out_shape=jax.ShapeDtypeStruct((SPAN, HD, x.shape[0]), bf),
        in_specs=[pl.BlockSpec(memory_space=pltpu.SMEM), v, v, v],
        out_specs=v,
        compiler_params=pltpu.CompilerParams(vmem_limit_bytes=32 << 20),
        cost_estimate=pl.CostEstimate(flops=3 * 10**8, bytes_accessed=2 << 20, transcendentals=0),
        name="cot_rows",
    )(first, x, own, other)


def heads_kernel(first_ref, x_ref, gain_ref, w_ref, cos_ref, sin_ref, *refs):
    buffer_ref, normed_ref = refs[-2:]
    x = x_ref[...].astype(f32)
    inverse = lax.rsqrt(jnp.mean(x * x, axis=-1, keepdims=True) + EPSILON)
    normed = (x * inverse * gain_ref[...]).astype(bf)
    normed_ref[...] = normed
    cosine, sine = cos_ref[...], sin_ref[...]
    heads = w_ref.shape[2] // HD
    first = first_ref[0]
    buffer_ref[...] = refs[0][...] if len(refs) == 3 else jnp.zeros(buffer_ref.shape, bf)
    for s in range(3):
        rows = dotf(normed, w_ref[s], 1, 0).T
        for h in range(heads):
            part = rows[h * HD : (h + 1) * HD]
            if s < 2:
                one, two = part[: HD // 2], part[HD // 2 :]
                part = jnp.concatenate([one * cosine - two * sine, two * cosine + one * sine], axis=0)
            buffer_ref[first + h, s * HD : (s + 1) * HD, :] = part.astype(bf)


def head_rows(first, x, gain, w, cosine, sine, buffer=None):
    half, width = x.shape
    v = pl.BlockSpec(memory_space=pltpu.VMEM)
    given = [] if buffer is None else [buffer]
    return pl.pallas_call(
        heads_kernel,
        out_shape=(
            jax.ShapeDtypeStruct((SPAN, 3 * HD, half), bf),
            jax.ShapeDtypeStruct((half, width), bf),
        ),
        in_specs=[pl.BlockSpec(memory_space=pltpu.SMEM)] + [v] * 5 + [v] * len(given),
        out_specs=(v, v),
        compiler_params=pltpu.CompilerParams(vmem_limit_bytes=40 << 20),
        cost_estimate=pl.CostEstimate(flops=5 * 10**8, bytes_accessed=4 << 20, transcendentals=0),
        name="head_rows",
    )(first, x, gain.reshape(1, width), w, cosine, sine, *given)


def head_grad_kernel(at_ref, dq_ref, dq_more_ref, own_ref, own_more_ref, other_ref, other_more_ref, cos_ref, sin_ref, *refs):
    pieces, grad_ref = refs[:-1], refs[-1]
    width = pieces[0].shape[-1]

    def back(rows, cosine, sine):
        one, two = rows[: HD // 2], rows[HD // 2 :]
        return jnp.concatenate([one * cosine + two * sine, two * cosine - one * sine], axis=0)

    acc = jnp.zeros((3 * HD, width), f32)
    n = 0
    for ref in pieces:
        for i in np.ndindex(*ref.shape[:-2]):
            block = at_ref[n]
            cosine, sine = cos_ref[block], sin_ref[block]
            split = own_ref.shape[0]
            one, two = jnp.minimum(block, split - 1), jnp.maximum(block - split, 0)
            dkv = jnp.where(
                block < split,
                own_ref[one] + other_ref[one].astype(f32),
                own_more_ref[two] + other_more_ref[two].astype(f32),
            )
            rows = jnp.concatenate(
                [back(dq_ref[block].astype(f32) + dq_more_ref[block].astype(f32), cosine, sine), back(dkv[:HD], cosine, sine), dkv[HD:]], axis=0
            ).astype(bf)
            grad_ref[block, 0 : 3 * HD, :] = rows
            acc = acc + dotf(rows, ref[i], 1, 0)
            n += 1
    turned = acc.T.astype(bf)
    blocks = grad_ref.shape[0]
    rows = width // blocks
    for block in range(blocks):
        grad_ref[block, 3 * HD :, :] = jnp.zeros((rows, grad_ref.shape[2]), bf)
        grad_ref[block, 3 * HD :, 0 : 3 * HD] = turned[block * rows : (block + 1) * rows]


def head_grad(at, dq, own, other, cosine, sine, pieces):
    v = pl.BlockSpec(memory_space=pltpu.VMEM)
    width = pieces[0].shape[-1]
    blocks, _, half = dq[0].shape
    return pl.pallas_call(
        head_grad_kernel,
        out_shape=jax.ShapeDtypeStruct((blocks, 3 * HD + width // blocks, half), bf),
        in_specs=[pl.BlockSpec(memory_space=pltpu.SMEM)] + [v] * (8 + len(pieces)),
        out_specs=v,
        compiler_params=pltpu.CompilerParams(vmem_limit_bytes=48 << 20),
        cost_estimate=pl.CostEstimate(flops=12 * 10**8, bytes_accessed=12 << 20, transcendentals=0),
        name="head_grad",
    )(at, *dq, *own, *other, cosine, sine, *pieces)


def swap(value, axis):
    return lax.ppermute(value, axis, [(0, 1), (1, 0)])


def plane_diagonal(value):
    return lax.ppermute(value, ("y", "x"), [(i, 3 - i) for i in range(4)])


def plane_gather(piece):
    mine = [piece, swap(piece, "x"), swap(piece, "y"), plane_diagonal(piece)]
    return mine + [swap(p, "t") for p in mine]


def plane_scatter(mine, other, before, later):
    other = swap(other, "t")
    held = [(mine[k].astype(f32) + other[k].astype(f32)).astype(bf) for k in range(4)]
    held, before, later = lax.optimization_barrier((held, before, later))
    parts = (held[0], swap(held[1], "x"), swap(held[2], "y"), plane_diagonal(held[3]))
    return sum(p.astype(f32) for p in parts), later


def over_z(value, distance):
    return lax.ppermute(value, "z", [(i, i ^ distance) for i in range(4)])


def chunk_of(chunks, at):
    return lax.dynamic_index_in_dim(chunks, jnp.clip(at, 0, 3), 0, keepdims=False)


def chain_send(sums, ahead, right, left):
    z = lax.axis_index("z")

    def joined(at, got):
        chunks = jnp.concatenate([chunk_of(chunks, at) for chunks in sums], axis=1)
        return (chunks.astype(f32) + got.astype(f32)).astype(bf)

    return joined(z + ahead, right), joined(z - ahead, left)


def chain_first(chunks):
    z = lax.axis_index("z")
    return chunk_of(chunks, jnp.where(z == 0, 3, 0))


def chain_ends(sent):
    return lax.ppermute(sent, "z", [(0, 1), (3, 2)])


def chain_move(sent, count):
    right = lax.ppermute(sent[0], "z", [(i, i + 1) for i in range(count)])
    left = lax.ppermute(sent[1], "z", [(3 - i, 2 - i) for i in range(count)])
    return right, left


def total(parts):
    first, rest = parts
    return first.astype(f32) + sum(p.astype(f32) for p in rest)


def plane_rows(chunks):
    b = lax.axis_index(("y", "x"))
    pick = lambda d: lax.dynamic_index_in_dim(chunks, b ^ d, 0, keepdims=False)
    return pick(0), [swap(pick(1), "x"), swap(pick(2), "y"), plane_diagonal(pick(3))]


def after(value, *others):
    return lax.optimization_barrier((value, others))[0]


def over_sequences(rows):
    if lax.axis_size("s") == 1:
        return rows
    return lax.psum_scatter(rows, "s", scatter_dimension=0, tiled=True)


def first_tokens(segments):
    def gathered(value, moved, places):
        low, high = places
        first = jnp.where(low == 0, jnp.stack([value, moved[0]]), jnp.stack([moved[0], value]))
        second = jnp.where(low == 0, jnp.stack([moved[1], moved[2]]), jnp.stack([moved[2], moved[1]]))
        return jnp.where(high == 0, jnp.stack([first, second]), jnp.stack([second, first]))

    z = lax.axis_index("z")
    plane = [swap(segments, "x"), swap(segments, "y"), plane_diagonal(segments)]
    ids = gathered(segments, plane, (lax.axis_index("x"), lax.axis_index("y"))).reshape(-1)
    ids = gathered(ids, [over_z(ids, d) for d in (1, 2, 3)], (z % 2, z // 2)).reshape(-1)
    count = ids.shape[0]
    index = jnp.arange(count, dtype=jnp.int32)
    before = jnp.concatenate([ids[:1], ids[:-1]])
    opens = jnp.where(ids != before, index, 0).reshape(-1, 256)
    n = opens.shape[0]
    lane = jnp.arange(256, dtype=jnp.int32)
    within = jnp.max(jnp.where(lane[None, None, :] <= lane[None, :, None], opens[:, None, :], 0), axis=-1)
    block = jnp.arange(n, dtype=jnp.int32)
    top = jnp.max(opens, axis=1)
    carry = jnp.max(jnp.where(block[None, :] < block[:, None], top[None, :], 0), axis=1)
    return jnp.maximum(within, carry[:, None]).reshape(-1)


def rotary_tables(position, half_dim):
    inv_freq = jnp.exp(jnp.arange(half_dim).astype(f32) * (-math.log(10000.0) / half_dim))
    phases = inv_freq[:, None] * position.astype(f32)[None, :]
    return jnp.cos(phases), jnp.sin(phases)


def rotate(values, cosine, sine):
    half_dim = values.shape[-2] // 2
    one, two = values[..., :half_dim, :], values[..., half_dim:, :]
    return jnp.concatenate([one * cosine - two * sine, two * cosine + one * sine], axis=-2)


def norm_forward(values, gain):
    inverse = lax.rsqrt(jnp.mean(values * values, axis=-1, keepdims=True) + EPSILON)
    return values * inverse * gain, inverse


def norm_backward(values, inverse, gain, upstream):
    scaled = upstream * gain
    inner = jnp.mean(scaled * values, axis=-1, keepdims=True)
    return (
        inverse * scaled - values * inverse * inverse * inverse * inner,
        jnp.sum(upstream * values * inverse, axis=0),
    )


def local(
    tokens,
    segments,
    routes,
    prev_logits,
    attn_gain,
    w_qkv,
    w_out,
    ffn_gain,
    w_router,
    w_const,
    v_const,
    w_gu,
    w_down,
    cotangent,
):
    tok_count, width = tokens.shape
    half = tok_count // 2
    features = w_qkv.shape[2]
    heads = features // HD
    t = lax.axis_index("t")
    place = lax.axis_index(GROUP)
    expert = lax.axis_index(("y", "x"))

    def mine(value):
        return lax.dynamic_slice_in_dim(value, t * half, half, 0)

    def both_halves(value):
        other = swap(value, "t")
        whole = jnp.zeros((tok_count,) + value.shape[1:], value.dtype)
        whole = lax.dynamic_update_slice_in_dim(whole, value, t * half, 0)
        return lax.dynamic_update_slice_in_dim(whole, other, (1 - t) * half, 0)

    w_qkv_other = swap(w_qkv, "t")
    w_out_other = swap(w_out, "t")
    inputs = mine(tokens).astype(f32)
    upstream_low = mine(cotangent)
    upstream = upstream_low.astype(f32)
    my_routes = jnp.transpose(mine(routes))
    my_prev = jnp.transpose(mine(prev_logits))
    kinds = jnp.arange(E_ALL, dtype=jnp.int32)[:, None]
    hot = (my_routes[0:1] == kinds).astype(f32) + (my_routes[1:2] == kinds).astype(f32)
    position = (place * tok_count + t * half + jnp.arange(half, dtype=jnp.int32)) % SEQ_LEN
    cosine, sine = rotary_tables(position, HD // 2)
    tokens_mine = mine(tokens)
    first = (t * heads).astype(jnp.int32).reshape(1)
    other_first = ((1 - t) * heads).astype(jnp.int32).reshape(1)
    buffer, normed_low = head_rows(first, tokens_mine, attn_gain, w_qkv, cosine, sine)
    buffer, _ = head_rows(other_first, tokens_mine, attn_gain, w_qkv_other, cosine, sine, buffer)

    def of_heads(buffer):
        return (
            lax.dynamic_slice_in_dim(buffer, t * heads, heads, 0),
            lax.dynamic_slice_in_dim(buffer, (1 - t) * heads, heads, 0),
        )

    def exchange(buffer):
        return lax.all_to_all(buffer, GROUP, 0, 0, tiled=True)

    upstream_sent, segments, buffer = lax.optimization_barrier((upstream_low, segments, buffer))
    start_all = first_tokens(segments)
    sc, start_rows = bounds(start_all, t, SPAN, half)
    own = exchange(buffer)
    oth = swap(own[:, HD:], "t")
    up_pieces = plane_gather(upstream_sent)
    expert_at = expert.astype(jnp.int32).reshape(1)
    normed_sent, own_q, up_pieces = lax.optimization_barrier((normed_low, own, up_pieces))
    along_z = [normed_sent] + [over_z(normed_sent, d) for d in (1, 2, 3)]
    heads_rows, heads_full, lse = flash_fwd(sc, start_rows, own_q, oth)
    heads_rows, along_z, up_pieces = lax.optimization_barrier((heads_rows, along_z, up_pieces))
    back = exchange(heads_rows)
    up_all, raw_all = hidden_cotangent(expert_at, up_pieces, w_down)
    back, raw_all = lax.optimization_barrier((back, raw_all))
    heads_own, heads_other = (v.reshape(features, half) for v in of_heads(back))
    branch = dotf(heads_own, w_out, 0, 0) + dotf(heads_other, w_out_other, 0, 0)
    residual = inputs + branch
    normed_ffn, inverse_ffn = norm_forward(residual, ffn_gain)
    ffn_low = normed_ffn.astype(bf)
    w_small = jnp.concatenate([w_router, w_const], axis=1)
    logits = dotf(w_small, ffn_low, 0, 1)
    router_probs = jax.nn.softmax(logits[:E_ALL] + my_prev, axis=0)
    expert_weight = router_probs * hot
    gate_rows = expert_weight[:E_FFN]
    gate_high = gate_rows.astype(bf)
    gate_low = (gate_rows - gate_high.astype(f32)).astype(bf)
    gate_block = jnp.pad(
        jnp.concatenate([gate_high, gate_low]), ((0, GATE_ROWS - 2 * E_FFN), (0, width - half))
    )
    x_all = plane_gather(jnp.concatenate([ffn_low, gate_block]))
    pair_a, pair_b = after((jnp.stack(along_z[:2]), jnp.stack(along_z[2:])), x_all)
    pair_ax, pair_by = swap(pair_a, "x"), swap(pair_b, "y")
    x_only, g_all, weighted, dx_mine, dx_other = expert_pass(expert_at, x_all, raw_all, w_gu)
    dx_mine, dx_other, pair_ax, pair_by = lax.optimization_barrier((dx_mine, dx_other, pair_ax, pair_by))
    hidden_units = w_down.shape[1]
    down_part = jnp.einsum("ptd,ptf->df", up_all, weighted, preferred_element_type=f32).astype(bf)
    received, (weighted, g_all) = plane_scatter(dx_mine, dx_other, down_part, (weighted, g_all))
    gu_part = jnp.einsum("ptd,ptf->df", x_only, g_all, preferred_element_type=f32).astype(bf)
    expert_part = over_sequences(jnp.concatenate([gu_part, down_part], axis=1))
    slab = expert_part.shape[0] // SPAN
    expert_part = expert_part.reshape(4, 4 * slab, 3 * hidden_units)
    expert_first = chain_first(expert_part)
    wdown_mine = lax.dynamic_index_in_dim(w_down, expert, 0, keepdims=False)
    out_mine = jnp.einsum("ptf,fd->ptd", weighted[:4], wdown_mine, preferred_element_type=f32).astype(bf)
    out_beside = jnp.einsum("ptf,fd->ptd", weighted[4:], wdown_mine, preferred_element_type=f32).astype(bf)
    received, expert_part, expert_first, out_mine, out_beside = lax.optimization_barrier(
        (received, expert_part, expert_first, out_mine, out_beside)
    )
    expert_got = chain_ends(expert_first)
    out_beside = swap(out_beside, "t")

    pairs = logits[E_ALL:].reshape(NCONST, 2, half)
    blend_one = jax.nn.sigmoid(pairs[:, 0] - pairs[:, 1])
    blend_two = jax.nn.sigmoid(pairs[:, 1] - pairs[:, 0])
    const_weight = expert_weight[E_FFN + 2 :]
    kept = expert_weight[E_FFN + 1 : E_FFN + 2] + jnp.sum(const_weight * blend_one, axis=0, keepdims=True)
    added = const_weight * blend_two
    columns = jnp.transpose(jnp.concatenate([kept, added]))
    kept_column, added_columns = columns[:, 0:1], columns[:, 1:]

    dx = received[:half]
    gating_ffn = received[half : half + E_FFN, :half]
    copy_dot = jnp.sum(upstream * normed_ffn, axis=-1)[None, :]
    vector_dot = lax.dot_general(v_const, upstream, (((1,), (1,)), ((), ())), precision=HIGHEST)
    const_dot = blend_one * copy_dot + blend_two * vector_dot
    dots = jnp.concatenate([gating_ffn, jnp.zeros((1, half), f32), copy_dot, const_dot])
    probs_grad = dots * hot
    prev_grad = router_probs * (probs_grad - jnp.sum(router_probs * probs_grad, axis=0, keepdims=True))
    grad_one = const_weight * copy_dot
    grad_two = const_weight * vector_dot
    inner = blend_one * grad_one + blend_two * grad_two
    const_grad = jnp.stack([blend_one * (grad_one - inner), blend_two * (grad_two - inner)], axis=1)
    logit_grad = jnp.concatenate([prev_grad, const_grad.reshape(2 * NCONST, half)])
    normed_grad = (
        dx
        + lax.dot_general(logit_grad, w_small.astype(f32), (((0,), (1,)), ((), ())), precision=HIGHEST)
        + kept_column * upstream
    )
    norm_grad, ffn_gain_part = norm_backward(residual, inverse_ffn, ffn_gain, normed_grad)
    residual_grad = upstream + norm_grad
    branch_cot = residual_grad.astype(bf)

    cot = cot_rows(jnp.concatenate([first, other_first]), branch_cot, w_out, w_out_other)
    small = jnp.concatenate(
        [
            ffn_gain_part[None],
            jnp.dot(logit_grad, ffn_low.astype(f32), precision=HIGHEST),
            jnp.dot(added, upstream, precision=HIGHEST),
        ]
    )
    small = jnp.transpose(jnp.pad(small, ((0, 128 - small.shape[0]), (0, 0)))).astype(bf)
    out_own = dotf(branch_cot, heads_own, 0, 1).astype(bf)
    out_other = dotf(branch_cot, heads_other, 0, 1).astype(bf)
    out_part = (out_own.astype(f32) + swap(out_other, "t").astype(f32)).astype(bf)
    out_part = over_sequences(jnp.concatenate([out_part, small], axis=1))
    out_part = out_part.reshape(4, 4 * slab, out_part.shape[1])
    got_out = chain_ends(chain_first(out_part))
    got = jnp.concatenate([expert_got, got_out], axis=1)
    sums = (expert_part, out_part)
    sent_parts = chain_send(sums, 2, got, got)
    held = [(out_mine[k].astype(f32) + out_beside[k].astype(f32)).astype(bf) for k in range(4)]

    t_late = after(t, heads_rows)
    all_position = (jnp.arange(SPAN, dtype=jnp.int32)[:, None] * tok_count + t_late * half)[:, :, None] + jnp.arange(half, dtype=jnp.int32)
    all_cosine, all_sine = rotary_tables(all_position.reshape(-1), HD // 2)
    by_block = lambda table: jnp.transpose(table.reshape(HD // 2, SPAN, half), (1, 0, 2))
    all_cosine, all_sine = by_block(all_cosine), by_block(all_sine)
    cot = exchange(cot)
    stack_a, stack_b = jnp.stack([pair_a, pair_ax]), jnp.stack([pair_b, pair_by])
    cot, held, stack_a, stack_b, sent_parts, all_cosine, all_sine = lax.optimization_barrier(
        (cot, held, stack_a, stack_b, sent_parts, all_cosine, all_sine)
    )
    pair_ya, pair_xb = swap(stack_a, "y"), swap(stack_b, "x")
    got = chain_move(sent_parts, 2)
    split = 5
    dq_one, own_one, oth_one = flash_bwd(sc, start_rows, own, oth, cot, heads_full, lse, 0, split)
    cot, oth_one, pair_ya, pair_xb, got = lax.optimization_barrier((cot, oth_one, pair_ya, pair_xb, got))
    oth_one = swap(oth_one, "t")
    sent_parts = chain_send(sums, 1, *got)
    cot, sent_parts, oth_one = lax.optimization_barrier((cot, sent_parts, oth_one))
    got = chain_move(sent_parts, 3)
    moved_out = [swap(held[1], "x"), swap(held[2], "y"), plane_diagonal(held[3])]
    dq_two, own_two, oth_two = flash_bwd(sc, start_rows, own, oth, cot, heads_full, lse, split, SPAN)
    oth_two, got, moved_out = lax.optimization_barrier((oth_two, got, moved_out))
    oth_two = swap(oth_two, "t")
    near = (0, 4, 8, 12, 1, 5, 10, 14, 2, 6, 3, 7, 9, 13, 11, 15)
    at = jnp.bitwise_xor(place, jnp.array(near, jnp.int32)).astype(jnp.int32)
    pieces = [pair_a, pair_b, pair_ax, pair_by, pair_ya, pair_xb]
    sent = head_grad(at, (dq_one, dq_two), (own_one, own_two), (oth_one, oth_two), all_cosine, all_sine, pieces)
    if lax.axis_size("s") > 1:
        head_part = over_sequences(sent[:, 3 * HD :, : 3 * HD].reshape(width, 3 * HD))
        head_part = jnp.pad(head_part.reshape(SPAN, slab, 3 * HD), ((0, 0), (0, 0), (0, half - 3 * HD)))
        sent = jnp.concatenate([sent[:, : 3 * HD], head_part], axis=1)
    sent, sums, got, held, moved_out, prev_grad, w_qkv, w_qkv_other = lax.optimization_barrier(
        (sent, sums, got, held, moved_out, prev_grad, w_qkv, w_qkv_other)
    )
    ffn_sum = sum(v.astype(f32) for v in [held[0]] + moved_out)
    arrived = exchange(sent)

    def feature_rows(w):
        return jnp.transpose(w.reshape(3, width, heads, HD), (2, 0, 3, 1)).reshape(3 * features, width)

    w_rows, w_rows_other = feature_rows(w_qkv), feature_rows(w_qkv_other)
    prev_both = both_halves(jnp.transpose(prev_grad))
    mixture = residual + ffn_sum + kept_column * normed_ffn + jnp.dot(added_columns, v_const, precision=HIGHEST)
    output = both_halves(mixture.astype(bf))
    kept_parts = jnp.concatenate([chunk_of(chunks, lax.axis_index("z")) for chunks in sums], axis=1)
    parts = (kept_parts.astype(f32) + got[0].astype(f32) + got[1].astype(f32)).astype(bf)
    parts = parts.reshape(4, slab, parts.shape[1])
    own_rows, got_rows = plane_rows(parts)
    columns_ffn = 3 * hidden_units
    ranks = jnp.bitwise_xor(expert, jnp.arange(4))
    by_distance = jnp.stack([rows[:, :columns_ffn] for rows in [own_rows] + got_rows])
    expert_rows = jnp.stack([lax.dynamic_index_in_dim(by_distance, ranks[k], 0, keepdims=False) for k in range(4)]).astype(f32)
    out_done = sum(rows[:, columns_ffn:].astype(f32) for rows in [own_rows] + got_rows)
    small = out_done[:, features:]
    small = small + swap(small, "t")
    w_gu_grad = jnp.transpose(
        expert_rows[:, :, : 2 * hidden_units].reshape(E_FFN, slab, 2, hidden_units), (0, 2, 1, 3)
    )
    w_down_grad = jnp.transpose(expert_rows[:, :, 2 * hidden_units :], (0, 2, 1))
    w_out_grad = jnp.transpose(out_done[:, :features])

    arrived, w_rows, w_rows_other, prev_both, output, w_gu_grad, w_down_grad, w_out_grad, small = (
        lax.optimization_barrier(
            (arrived, w_rows, w_rows_other, prev_both, output, w_gu_grad, w_down_grad, w_out_grad, small)
        )
    )
    arrived_own, arrived_other = of_heads(arrived)
    back_own, back_other = arrived_own[:, : 3 * HD], arrived_other[:, : 3 * HD]
    part_own, part_other = arrived_own[:, 3 * HD :, : 3 * HD], arrived_other[:, 3 * HD :, : 3 * HD]
    head_sum = part_own.astype(f32) + swap(part_other, "t").astype(f32)
    w_qkv_grad = jnp.transpose(head_sum.reshape(heads, slab, 3, HD), (2, 1, 0, 3)).reshape(3, slab, features)
    d_first = (lax.axis_index("s") * SPAN + place) * slab
    w_slab = lax.dynamic_slice_in_dim(w_qkv, d_first, slab, 1).astype(f32)
    gain_part = jnp.sum(w_slab * w_qkv_grad, axis=(0, 2))
    attn_gain_grad = (gain_part + swap(gain_part, "t")) / lax.dynamic_slice_in_dim(attn_gain, d_first, slab, 0)

    grad_own, grad_other = (v.reshape(3 * features, half) for v in (back_own, back_other))
    attn_grad = dotf(grad_own, w_rows, 0, 0) + dotf(grad_other, w_rows_other, 0, 0)
    inverse_attn = lax.rsqrt(jnp.mean(inputs * inputs, axis=-1, keepdims=True) + EPSILON)
    token_norm_grad, _ = norm_backward(inputs, inverse_attn, attn_gain, attn_grad)
    tokens_grad = both_halves(residual_grad + token_norm_grad)
    return (
        output,
        tokens_grad,
        prev_both,
        attn_gain_grad,
        w_qkv_grad,
        w_out_grad,
        small[:, 0],
        small[:, 1 : 1 + E_ALL],
        small[:, 9 : 9 + 2 * NCONST],
        jnp.transpose(small[:, 13 : 13 + NCONST]),
        w_gu_grad,
        w_down_grad,
    )


def solution(mesh):
    dp = mesh.shape["dp"]
    devices = mesh.devices.reshape(dp // SPAN, 4, 2, 2, mesh.shape["tensor"])
    inner = Mesh(devices, ("s", "z", "y", "x", "t"))
    d = ("s", "z", "y", "x")
    return jax.shard_map(
        local,
        mesh=inner,
        in_specs=(
            P(d, None),
            P(d),
            P(d, None),
            P(d, None),
            P(),
            P(None, None, "t"),
            P("t", None),
            P(),
            P(),
            P(),
            P(),
            P(None, None, None, "t"),
            P(None, "t", None),
            P(d, None),
        ),
        out_specs=(
            P(d, None),
            P(d, None),
            P(d, None),
            P(d),
            P(None, d, "t"),
            P("t", d),
            P(d),
            P(d, None),
            P(d, None),
            P(None, d),
            P(None, None, d, "t"),
            P(None, "t", d),
        ),
        check_vma=False,
    )
```

time: 3070 us -> 491 us (0.16)
  waiting for transfers between devices: 1420 us -> 67.9 us
  local copies, waits for them, and re-layouts: 620 us -> 70.2 us
  matrix products: 582 us -> 34.4 us
  Pallas kernels: 0 us -> 152 us
  starting transfers between devices: 231 us -> 108 us
  other arithmetic: 93.2 us -> 37.9 us
  loops' own time: 47.5 us -> 0 us
  blocking collectives: 31 us -> 0 us
    reduce_scatter x3 -> x0, waiting for transfers between devices: 705 us -> none  [the longest x1 367 us: local(): lax.psum_scatter(w_gu_local, 'dp', scatter_dimension=2, tiled=True)]
    dot_general x179 -> x16, matrix products: 576 us -> 34.4 us  [the longest x1 7.31 us: local(): jnp.einsum('ptd,ptf->df', x_only, g_all, preferred_element_type=f32)]
    unnamed x14 -> x0, waiting for transfers between devices: 275 us -> none
    another operation x54 -> x6, local copies, waits for them, and re-layouts: 257 us -> 3.7 us  [the longest x4 3.67 us: local(): jnp.stack([rows[:, :columns_ffn] for rows in [own_rows] + got_rows])]
    ppermute x75 -> x56, waiting for transfers between devices: 316 us -> 67.9 us  [the longest x38 27.8 us: swap(): return lax.ppermute(value, axis, [(0, 1), (1, 0)])]
    scatter-add x48 -> x0, local copies, waits for them, and re-layouts: 212 us -> none  [the longest x24 119 us: grad_scan(): gu_total = gu_total.at[operand[4]].add(gu_step)]
    pallas_call x0 -> x9, Pallas kernels: none -> 152 us  [the longest x2 69.7 us: flash_bwd(): pl.pallas_call(functools.partial(bwd_kernel, nb, half, j0, j1), out_shape...]
    ppermute x75 -> x56, starting transfers between devices: 230 us -> 79.2 us  [the longest x38 50.1 us: swap(): return lax.ppermute(value, axis, [(0, 1), (1, 0)])]
  transfers between devices with their start and end apart: 85 -> 60, of which waited for: 33 -> 14; matrix products, arithmetic and copies ran while one was open for 11% -> 22% of each run, Pallas kernels for 0% -> 30%
where the time goes in v1:
time: 491 us; the launch traced here: 481 us
  Pallas kernels  152 us (31%)
  starting transfers between devices  108 us (22%)
  local copies, waits for them, and re-layouts  70.2 us (14%)
  waiting for transfers between devices  67.9 us (14%)
  other arithmetic  37.9 us (8%)
  matrix products  34.4 us (7%)
  between operations  10.5 us (2%)
    pallas_call x2, Pallas kernels, flash_bwd(): pl.pallas_call(functools.partial(bwd_kernel, nb, half, j0, j1), out_shape...  69.7 us
    ppermute x38, starting transfers between devices, swap(): return lax.ppermute(value, axis, [(0, 1), (1, 0)])  50.1 us
    pallas_call x1, Pallas kernels, flash_fwd(): pl.pallas_call(functools.partial(fwd_kernel, nb, half), out_shape=(jax.Sh...  38.2 us
    all_to_all x4, starting transfers between devices, exchange(): return lax.all_to_all(buffer, GROUP, 0, 0, tiled=True)  28.7 us
    ppermute x38, waiting for transfers between devices, swap(): return lax.ppermute(value, axis, [(0, 1), (1, 0)])  27.8 us
    pallas_call x1, Pallas kernels, expert_pass(): pl.pallas_call(ffn_kernel, out_shape=(jax.ShapeDtypeStruct((8, half, widt...  26.1 us
    unnamed x233, local copies, waits for them, and re-layouts  25.5 us
    ppermute x6, waiting for transfers between devices, over_z(): return lax.ppermute(value, 'z', [(i, i ^ distance) for i in range(4)])  23.4 us
  transfers between devices with their start and end apart: 60, of which 14 were waited for; matrix products, arithmetic and copies ran while one was open for 22% of the time, Pallas kernels for 30%

profile of v1, /device:TPU:17, one launch (start us, length us, event | category | flops | bytes accessed | tf_op | source)
XLA Modules:
  0.0 480.8 jit_solution(11045151371249968370)
XLA Ops:
  3.4 1.5 copy-done.2
  7.0 1.6 head_rows.3
  9.8 6.7 %all-to-all-start = ((bf16[16,192,256]{2,1,0:T(8,128)(2,1)}), bf16[16,192,256]{2,1,0:T(8,128)(2,1)S(1)}, u32[]{:S(2)}, u32[]{:S(2)}) async-start(bf16[16,192,256]{2,1,0:T(8,128)(2,1)} %copy-done.13), calls=%async_computation | async-start | bytes 3145728 | tf_op jit(solution)/shard_map/all_to_all | solution.py:692
  24.9 5.9 %collective-permute-start.5 = (s32[2048]{0:T(1024)S(1)}, s32[2048]{0:T(1024)S(1)}, u32[]{:S(2)}, u32[]{:S(2)}) collective-permute-start(s32[2048]{0:T(1024)S(1)} %bitcast.251), channel_id=1, source_target_pairs={{0,16},{8,24},{16,0},{24,8},{1,17},{9,25},{17,1},{25,9},{2,18},{10... | collective-permute-start | bytes 24584 | tf_op jit(solution)/shard_map/ppermute | solution.py:532
  30.9 21.2 %collective-permute-done.6 = s32[2048]{0:T(1024)S(1)} collective-permute-done((s32[2048]{0:T(1024)S(1)}, s32[2048]{0:T(1024)S(1)}, u32[]{:S(2)}, u32[]{:S(2)}) %collective-permute-start.6) | collective-permute-done | bytes 8224 | tf_op jit(solution)/shard_map/ppermute | solution.py:532
  53.4 2.2 collective-permute-done.4
  64.7 1.3 collective-permute-start.15
  67.8 38.2 %flash_fwd.1 = (bf16[16,64,256]{2,1,0:T(8,128)(2,1)}, f32[16,64,256]{2,1,0:T(8,128)S(1)}, f32[16,1,256]{2,1,0:T(1,128)S(1)}) custom-call(s32[65]{0:T(128)S(1)} %concatenate.115.sc, s32[16,1,256]{2,1,0:T(1,128)S(1)} %dynamic-slice_maximum_fusion.start_ref, bf16[16,192,256]{2,1,0:T(8,128)(2,1)S(1)} %all-to-all-done.own_ref, ...), custom_call_target="tpu_custom_call" | custom-call | flops 1000000000 | bytes 4194304 | tf_op jit(solution)/shard_map/flash_fwd/pallas_call | solution.py:119
  107.6 8.8 %all-to-all-start.1 = ((bf16[16,64,256]{2,1,0:T(8,128)(2,1)}), bf16[16,64,256]{2,1,0:T(8,128)(2,1)S(1)}, u32[]{:S(2)}, u32[]{:S(2)}) async-start(bf16[16,64,256]{2,1,0:T(8,128)(2,1)} %get-tuple-element.142), calls=%async_computation.1 | async-start | bytes 1048576 | tf_op jit(solution)/shard_map/all_to_all | solution.py:692
  117.1 7.7 %hidden_cotangent.1 = (bf16[8,256,768]{2,1,0:T(8,128)(2,1)S(1)}, bf16[8,256,1024]{2,1,0:T(8,128)(2,1)S(1)}) custom-call(s32[1]{0:T(128)} %bitcast.10.e_ref, bf16[4,1024,768]{2,1,0:T(8,128)(2,1)} %w_ref.3, bf16[256,768]{1,0:T(8,128)(2,1)S(1)} %constant_dynamic-slice_fusion.13.refs_0_, bf16[256,768]{1,0:T(8,128)(2,1)} %collective-permute-done.8.refs_1_, ...), custom_call_target="tpu_custom_call" | custom-call | flops 3200000000 | bytes 12582912 | tf_op jit(solution)/shard_map/hidden_cotangent/pallas_call | solution.py:376
  124.9 2.0 copy-done.24
  126.9 1.7 copy-done.25
  129.2 1.6 multiply_reduce_fusion.2
  137.3 2.8 multiply_sine_fusion
  140.1 6.3 %collective-permute-start.22 = (bf16[272,768]{1,0:T(8,128)(2,1)S(1)}, bf16[272,768]{1,0:T(8,128)(2,1)S(1)}, u32[]{:S(2)}, u32[]{:S(2)}) collective-permute-start(bf16[272,768]{1,0:T(8,128)(2,1)S(1)} %pad_maximum_fusion.8.refs_0_), channel_id=1, source_target_pairs={{0,1},{1,0},{2,3},{3,2},{4,5},{5,4},{6,7},{7,6},{8,9},{9,8},{10,11... | collective-permute-start | bytes 1253384 | tf_op jit(solution)/shard_map/ppermute | solution.py:511
  146.4 2.5 collective-permute-start.23
  149.0 5.6 %collective-permute-start.24 = (bf16[272,768]{1,0:T(8,128)(2,1)}, bf16[272,768]{1,0:T(8,128)(2,1)S(1)}, u32[]{:S(2)}, u32[]{:S(2)}) collective-permute-start(bf16[272,768]{1,0:T(8,128)(2,1)} %collective-permute-done.20.refs_2_), channel_id=1, source_target_pairs={{0,1},{1,0},{2,3},{3,2},{4,5},{5,4},{6,7},{7,6},{8,9},{9,8},{10,11... | collective-permute-start | bytes 1253384 | tf_op jit(solution)/shard_map/ppermute | solution.py:511
  160.3 26.1 %expert_pass.1 = (bf16[8,256,768]{2,1,0:T(8,128)(2,1)}, bf16[8,256,2048]{2,1,0:T(8,128)(2,1)}, bf16[8,256,1024]{2,1,0:T(8,128)(2,1)}, bf16[4,272,768]{2,1,0:T(8,128)(2,1)S(1)}, bf16[4,272,768]{2,1,0:T(8,128)(2,1)}) custom-call(s32[1]{0:T(128)} %bitcast.10.e_ref, bf16[8,256,1024]{2,1,0:T(8,128)(2,1)} %copy-done.24, bf16[4,2,768,1024]{3,2,1,0:T(8,128)(2,1)} %wgu_ref.1, ...), custom_call_target="tpu_custom_call" | custom-call | flops 12884901888 | bytes 41943040 | tf_op jit(solution)/shard_map/expert_pass/pallas_call | solution.py:328
  191.8 7.2 %bitcast_convert_fusion.1 = bf16[768,1024]{1,0:T(8,128)(2,1)S(1)} fusion(bf16[8,256,768]{2,1,0:T(8,128)(2,1)} %copy-done.25, bf16[8,256,1024]{2,1,0:T(8,128)(2,1)} %get-tuple-element.173), kind=kOutput, calls=%fused_computation.5 | convolution fusion | flops 3222011904 | bytes 8912896 | tf_op jit(solution)/shard_map/ptd,ptf->df/dot_general | solution.py:729
  199.0 1.9 fusion.21
  203.7 7.3 %bitcast_convert_fusion = bf16[768,2048]{1,0:T(8,128)(2,1)S(1)} fusion(bf16[8,256,768]{2,1,0:T(8,128)(2,1)S(1)} %copy-done.108, bf16[8,256,2048]{2,1,0:T(8,128)(2,1)S(1)} %bitcast.264), kind=kOutput, calls=%fused_computation.1 | convolution fusion | flops 6444023808 | bytes 14680064 | tf_op jit(solution)/shard_map/ptd,ptf->df/dot_general | solution.py:731
  212.7 5.4 %convolution_convert_fusion.1 = bf16[4,256,768]{2,1,0:T(8,128)(2,1)} fusion(bf16[8,256,1024]{2,1,0:T(8,128)(2,1)} %get-tuple-element.173, bf16[4,1024,768]{2,1,0:T(8,128)(2,1)S(1)} %bitcast.262, s32[]{:T(128)S(6)} %select_n.257), kind=kOutput, calls=%fused_computation.12 | convolution fusion | flops 1611399168 | bytes 7340036 | tf_op jit(solution)/shard_map/ptf,fd->ptd/dot_general | solution.py:737
  218.1 3.0 convolution_convert_fusion
  221.1 1.4 collective-permute-done.30
  223.0 1.3 multiply_reduce_fusion
  227.0 1.3 pad_maximum_fusion.1
  228.4 1.4 pad_maximum_fusion.2
  229.8 1.3 collective-permute-start.34
  232.0 1.6 cot_rows.1
  234.4 7.4 %all-to-all-start.2 = ((bf16[16,64,256]{2,1,0:T(8,128)(2,1)}), bf16[16,64,256]{2,1,0:T(8,128)(2,1)}, u32[]{:S(2)}, u32[]{:S(2)}) async-start(bf16[16,64,256]{2,1,0:T(8,128)(2,1)} %copy-done.8), calls=%async_computation.2 | async-start | bytes 1048576 | tf_op jit(solution)/shard_map/all_to_all | solution.py:692
  243.4 1.4 add_convert_fusion.3
  245.7 2.3 copy.74
  248.0 2.1 dynamic-slice_bitcast_fusion.11
  250.1 1.3 collective-permute-start.35
  251.4 4.0 dynamic-slice_bitcast_fusion.1
  255.5 16.6 %collective-permute-done.35 = bf16[192,512]{1,0:T(8,128)(2,1)S(1)} collective-permute-done((bf16[192,512]{1,0:T(8,128)(2,1)S(1)}, bf16[192,512]{1,0:T(8,128)(2,1)S(1)}, u32[]{:S(2)}, u32[]{:S(2)}) %collective-permute-start.35) | collective-permute-done | bytes 196640 | tf_op jit(solution)/shard_map/ppermute | solution.py:555
  272.1 3.5 fusion.1
  275.6 2.6 fusion.25
  279.7 1.3 collective-permute-start.38
  281.0 4.0 collective-permute-start.39
  285.0 35.6 %flash_bwd.2 = (bf16[16,64,256]{2,1,0:T(8,128)(2,1)}, f32[5,128,256]{2,1,0:T(8,128)}, bf16[5,128,256]{2,1,0:T(8,128)(2,1)}) custom-call(s32[65]{0:T(128)} %copy-done.21, s32[16,1,256]{2,1,0:T(1,128)} %copy-done.19, bf16[16,192,256]{2,1,0:T(8,128)(2,1)} %copy-done.1, bf16[16,128,256]{2,1,0:T(8,128)(2,1)} %collective-permute-done.7.oth_ref, ...), custom_call_target="tpu_custom_call" | custom-call | flops 1000000000 | bytes 4194304 | tf_op jit(solution)/shard_map/flash_bwd/pallas_call | solution.py:225
  320.7 4.9 %collective-permute-start.40 = (bf16[5,128,256]{2,1,0:T(8,128)(2,1)}, bf16[5,128,256]{2,1,0:T(8,128)(2,1)S(1)}, u32[]{:S(2)}, u32[]{:S(2)}) collective-permute-start(bf16[5,128,256]{2,1,0:T(8,128)(2,1)} %get-tuple-element.194), channel_id=1, source_target_pairs={{0,1},{1,0},{2,3},{3,2},{4,5},{5,4},{6,7},{7,6},{8,9},{9,8},{10,11... | collective-permute-start | bytes 983048 | tf_op jit(solution)/shard_map/ppermute | solution.py:511
  325.6 3.0 add_convert_fusion.2
  328.7 1.8 add_convert_fusion.1
  330.5 2.1 collective-permute-start.41
  332.6 3.1 collective-permute-start.42
  338.5 34.1 %flash_bwd.3 = (bf16[16,64,256]{2,1,0:T(8,128)(2,1)}, f32[11,128,256]{2,1,0:T(8,128)}, bf16[11,128,256]{2,1,0:T(8,128)(2,1)}) custom-call(s32[65]{0:T(128)} %copy-done.21, s32[16,1,256]{2,1,0:T(1,128)} %copy-done.19, bf16[16,192,256]{2,1,0:T(8,128)(2,1)} %copy-done.1, bf16[16,128,256]{2,1,0:T(8,128)(2,1)} %collective-permute-done.7.oth_ref, ...), custom_call_target="tpu_custom_call" | custom-call | flops 1000000000 | bytes 4194304 | tf_op jit(solution)/shard_map/flash_bwd/pallas_call | solution.py:225
  373.6 8.3 %collective-permute-start.46 = (bf16[11,128,256]{2,1,0:T(8,128)(2,1)}, bf16[11,128,256]{2,1,0:T(8,128)(2,1)}, u32[]{:S(2)}, u32[]{:S(2)}) collective-permute-start(bf16[11,128,256]{2,1,0:T(8,128)(2,1)} %get-tuple-element.206), channel_id=1, source_target_pairs={{0,1},{1,0},{2,3},{3,2},{4,5},{5,4},{6,7},{7,6},{8,9},{9,8},{10,11... | collective-permute-start | bytes 2162696 | tf_op jit(solution)/shard_map/ppermute | solution.py:511
  390.3 1.7 fusion.46
  397.3 6.0 %head_grad.1 = bf16[16,240,256]{2,1,0:T(8,128)(2,1)} custom-call(s32[16]{0:T(128)S(1)} %broadcast_xor_fusion.at_ref, bf16[16,64,256]{2,1,0:T(8,128)(2,1)S(1)} %copy-done.15, bf16[16,64,256]{2,1,0:T(8,128)(2,1)S(1)} %copy-done.16, f32[5,128,256]{2,1,0:T(8,128)S(1)} %copy-done.14, f32[11,128,256]{2,1,0:T(8,128)} %get-tuple-element.198.own_more_ref, ...), custom_call_target="tpu_custom_call" | custom-call | flops 1200000000 | bytes 12582912 | tf_op jit(solution)/shard_map/head_grad/pallas_call | solution.py:499
  403.3 5.9 %all-to-all-start.3 = ((bf16[16,240,256]{2,1,0:T(8,128)(2,1)}), bf16[16,240,256]{2,1,0:T(8,128)(2,1)}, u32[]{:S(2)}, u32[]{:S(2)}) async-start(bf16[16,240,256]{2,1,0:T(8,128)(2,1)} %head_grad.1), calls=%async_computation.3 | async-start | bytes 3932160 | tf_op jit(solution)/shard_map/all_to_all | solution.py:692
  410.8 1.4 dynamic-slice_bitcast_fusion
  412.1 2.3 add_convert_fusion
  415.6 2.1 collective-permute-start.51
  419.9 1.3 constant_dynamic-update-slice_fusion.3
  421.6 2.3 copy.75
  423.9 2.9 copy.76
  426.7 3.8 copy.77
  430.6 2.9 copy.78
  434.4 8.8 %collective-permute-done.50 = bf16[48,3584]{1,0:T(8,128)(2,1)} collective-permute-done((bf16[48,3584]{1,0:T(8,128)(2,1)}, bf16[48,3584]{1,0:T(8,128)(2,1)}, u32[]{:S(2)}, u32[]{:S(2)}) %collective-permute-start.50) | collective-permute-done | bytes 344096 | tf_op jit(solution)/shard_map/ppermute | solution.py:511
  443.2 12.0 %collective-permute-done.49 = bf16[48,3584]{1,0:T(8,128)(2,1)} collective-permute-done((bf16[48,3584]{1,0:T(8,128)(2,1)}, bf16[48,3584]{1,0:T(8,128)(2,1)}, u32[]{:S(2)}, u32[]{:S(2)}) %collective-permute-start.49) | collective-permute-done | bytes 344096 | tf_op jit(solution)/shard_map/ppermute | solution.py:511
  464.3 1.4 constant_dynamic-slice_fusion.1
  469.7 1.4 constant_dynamic-update-slice_fusion.1
  478.3 2.1 constant_dynamic-update-slice_fusion
  (449 shorter events, 95.7 us)
Async XLA Ops:
  0.6 154.0 %copy-start = (f32[2,768]{1,0:T(2,128)S(1)}, f32[2,768]{1,0:T(2,128)}, u32[]{:S(2)}) copy-start(f32[2,768]{1,0:T(2,128)} %param.25) | copy-start | bytes 18436
  0.7 6.3 %collective-permute-start = (bf16[3,768,384]{2,1,0:T(8,128)(2,1)}, bf16[3,768,384]{2,1,0:T(8,128)(2,1)S(1)}, u32[]{:S(2)}, u32[]{:S(2)}) collective-permute-start(bf16[3,768,384]{2,1,0:T(8,128)(2,1)} %w_ref.2), channel_id=1, source_target_pairs={{0,1},{1,0},{2,3},{3,2},{4,5},{5,4},{6,7},{7,6},{8,9},{9,8},{10,11... | collective-permute-start | bytes 5308424 | tf_op jit(solution)/shard_map/ppermute | solution.py:511
  9.8 47.6 %all-to-all-start = ((bf16[16,192,256]{2,1,0:T(8,128)(2,1)}), bf16[16,192,256]{2,1,0:T(8,128)(2,1)S(1)}, u32[]{:S(2)}, u32[]{:S(2)}) async-start(bf16[16,192,256]{2,1,0:T(8,128)(2,1)} %copy-done.13), calls=%async_computation | async-start | bytes 3145728 | tf_op jit(solution)/shard_map/all_to_all | solution.py:692
  16.5 6.1 %collective-permute-start.1 = (s32[512]{0:T(512)S(1)}, s32[512]{0:T(512)S(1)}, u32[]{:S(2)}, u32[]{:S(2)}) collective-permute-start(s32[512]{0:T(512)S(1)} %copy-done.103), channel_id=1, source_target_pairs={{0,2},{2,0},{1,3},{3,1},{4,6},{6,4},{5,7},{7,5},{8,10},{10,8},{9,1... | collective-permute-start | bytes 6152 | tf_op jit(solution)/shard_map/ppermute | solution.py:511
  17.8 6.0 %collective-permute-start.3 = (s32[512]{0:T(512)S(1)}, s32[512]{0:T(512)S(1)}, u32[]{:S(2)}, u32[]{:S(2)}) collective-permute-start(s32[512]{0:T(512)S(1)} %copy-done.103), channel_id=1, source_target_pairs={{0,6},{2,4},{4,2},{6,0},{1,7},{3,5},{5,3},{7,1},{8,14},{10,12},{12... | collective-permute-start | bytes 6152 | tf_op jit(solution)/shard_map/ppermute | solution.py:515
  19.0 5.8 %collective-permute-start.2 = (s32[512]{0:T(512)S(1)}, s32[512]{0:T(512)S(1)}, u32[]{:S(2)}, u32[]{:S(2)}) collective-permute-start(s32[512]{0:T(512)S(1)} %copy-done.103), channel_id=1, source_target_pairs={{0,4},{4,0},{1,5},{5,1},{2,6},{6,2},{3,7},{7,3},{8,12},{12,8},{9,1... | collective-permute-start | bytes 6152 | tf_op jit(solution)/shard_map/ppermute | solution.py:511
  19.3 41.6 %collective-permute-start.8 = (bf16[256,768]{1,0:T(8,128)(2,1)S(1)}, bf16[256,768]{1,0:T(8,128)(2,1)}, u32[]{:S(2)}, u32[]{:S(2)}) collective-permute-start(bf16[256,768]{1,0:T(8,128)(2,1)S(1)} %constant_dynamic-slice_fusion.13.refs_0_), channel_id=1, source_target_pairs={{0,2},{2,0},{1,3},{3,1},{4,6},{6,4},{5,7},{7,5},{8,10},{10,8},{9,1... | collective-permute-start | bytes 1179656 | tf_op jit(solution)/shard_map/ppermute | solution.py:511
  20.4 40.5 %collective-permute-start.9 = (bf16[256,768]{1,0:T(8,128)(2,1)S(1)}, bf16[256,768]{1,0:T(8,128)(2,1)}, u32[]{:S(2)}, u32[]{:S(2)}) collective-permute-start(bf16[256,768]{1,0:T(8,128)(2,1)S(1)} %constant_dynamic-slice_fusion.13.refs_0_), channel_id=1, source_target_pairs={{0,4},{4,0},{1,5},{5,1},{2,6},{6,2},{3,7},{7,3},{8,12},{12,8},{9,1... | collective-permute-start | bytes 1179656 | tf_op jit(solution)/shard_map/ppermute | solution.py:511
  22.6 38.9 %collective-permute-start.10 = (bf16[256,768]{1,0:T(8,128)(2,1)S(1)}, bf16[256,768]{1,0:T(8,128)(2,1)}, u32[]{:S(2)}, u32[]{:S(2)}) collective-permute-start(bf16[256,768]{1,0:T(8,128)(2,1)S(1)} %constant_dynamic-slice_fusion.13.refs_0_), channel_id=1, source_target_pairs={{0,6},{2,4},{4,2},{6,0},{1,7},{3,5},{5,3},{7,1},{8,14},{10,12},{12... | collective-permute-start | bytes 1179656 | tf_op jit(solution)/shard_map/ppermute | solution.py:515
  24.9 27.2 %collective-permute-start.6 = (s32[2048]{0:T(1024)S(1)}, s32[2048]{0:T(1024)S(1)}, u32[]{:S(2)}, u32[]{:S(2)}) collective-permute-start(s32[2048]{0:T(1024)S(1)} %bitcast.250), channel_id=1, source_target_pairs={{0,24},{8,16},{16,8},{24,0},{1,25},{9,17},{17,9},{25,1},{2,26},{10... | collective-permute-start | bytes 24584 | tf_op jit(solution)/shard_map/ppermute | solution.py:532
  24.9 28.2 %collective-permute-start.5 = (s32[2048]{0:T(1024)S(1)}, s32[2048]{0:T(1024)S(1)}, u32[]{:S(2)}, u32[]{:S(2)}) collective-permute-start(s32[2048]{0:T(1024)S(1)} %bitcast.251), channel_id=1, source_target_pairs={{0,16},{8,24},{16,0},{24,8},{1,17},{9,25},{17,1},{25,9},{2,18},{10... | collective-permute-start | bytes 24584 | tf_op jit(solution)/shard_map/ppermute | solution.py:532
  52.0 9.9 %collective-permute-start.11 = (bf16[256,768]{1,0:T(8,128)(2,1)S(1)}, bf16[256,768]{1,0:T(8,128)(2,1)}, u32[]{:S(2)}, u32[]{:S(2)}) collective-permute-start(bf16[256,768]{1,0:T(8,128)(2,1)S(1)} %constant_dynamic-slice_fusion.13.refs_0_), channel_id=1, source_target_pairs={{0,1},{1,0},{2,3},{3,2},{4,5},{5,4},{6,7},{7,6},{8,9},{9,8},{10,11... | collective-permute-start | bytes 1179656 | tf_op jit(solution)/shard_map/ppermute | solution.py:511
  53.2 2.5 collective-permute-start.4
  58.5 9.3 %collective-permute-start.7 = (bf16[16,128,256]{2,1,0:T(8,128)(2,1)}, bf16[16,128,256]{2,1,0:T(8,128)(2,1)}, u32[]{:S(2)}, u32[]{:S(2)}) collective-permute-start(bf16[16,128,256]{2,1,0:T(8,128)(2,1)} %slice.246), channel_id=1, source_target_pairs={{0,1},{1,0},{2,3},{3,2},{4,5},{5,4},{6,7},{7,6},{8,9},{9,8},{10,11... | collective-permute-start | bytes 3145736 | tf_op jit(solution)/shard_map/ppermute | solution.py:511
  60.9 2.1 collective-permute-start.12
  61.0 2.6 collective-permute-start.13
  61.5 3.2 collective-permute-start.14
  62.0 67.2 %collective-permute-start.18 = (bf16[384,768]{1,0:T(8,128)(2,1)S(1)}, bf16[384,768]{1,0:T(8,128)(2,1)}, u32[]{:S(2)}, u32[]{:S(2)}) collective-permute-start(bf16[384,768]{1,0:T(8,128)(2,1)S(1)} %copy-done.6), channel_id=1, source_target_pairs={{0,1},{1,0},{2,3},{3,2},{4,5},{5,4},{6,7},{7,6},{8,9},{9,8},{10,11... | collective-permute-start | bytes 1769480 | tf_op jit(solution)/shard_map/ppermute | solution.py:511
  64.7 42.8 %collective-permute-start.15 = (bf16[256,768]{1,0:T(8,128)(2,1)S(1)}, bf16[256,768]{1,0:T(8,128)(2,1)}, u32[]{:S(2)}, u32[]{:S(2)}) collective-permute-start(bf16[256,768]{1,0:T(8,128)(2,1)S(1)} %get-tuple-element.156), channel_id=1, source_target_pairs={{0,8},{8,0},{16,24},{24,16},{1,9},{9,1},{17,25},{25,17},{2,10},{10... | collective-permute-start | bytes 1179656 | tf_op jit(solution)/shard_map/ppermute | solution.py:532
  66.0 41.6 %collective-permute-start.16 = (bf16[256,768]{1,0:T(8,128)(2,1)S(1)}, bf16[256,768]{1,0:T(8,128)(2,1)}, u32[]{:S(2)}, u32[]{:S(2)}) collective-permute-start(bf16[256,768]{1,0:T(8,128)(2,1)S(1)} %get-tuple-element.156), channel_id=1, source_target_pairs={{0,16},{8,24},{16,0},{24,8},{1,17},{9,25},{17,1},{25,9},{2,18},{10... | collective-permute-start | bytes 1179656 | tf_op jit(solution)/shard_map/ppermute | solution.py:532
  67.1 40.4 %collective-permute-start.17 = (bf16[256,768]{1,0:T(8,128)(2,1)S(1)}, bf16[256,768]{1,0:T(8,128)(2,1)}, u32[]{:S(2)}, u32[]{:S(2)}) collective-permute-start(bf16[256,768]{1,0:T(8,128)(2,1)S(1)} %get-tuple-element.156), channel_id=1, source_target_pairs={{0,24},{8,16},{16,8},{24,0},{1,25},{9,17},{17,9},{25,1},{2,26},{10... | collective-permute-start | bytes 1179656 | tf_op jit(solution)/shard_map/ppermute | solution.py:532
  67.8 49.3 %copy-start.99 = (bf16[768,4]{0,1:T(4,128)(2,1)S(1)}, bf16[768,4]{0,1:T(4,128)(2,1)}, u32[]{:S(2)}) copy-start(bf16[768,4]{0,1:T(4,128)(2,1)} %param.24) | copy-start | bytes 18436
  107.6 21.1 %all-to-all-start.1 = ((bf16[16,64,256]{2,1,0:T(8,128)(2,1)}), bf16[16,64,256]{2,1,0:T(8,128)(2,1)S(1)}, u32[]{:S(2)}, u32[]{:S(2)}) async-start(bf16[16,64,256]{2,1,0:T(8,128)(2,1)} %get-tuple-element.142), calls=%async_computation.1 | async-start | bytes 1048576 | tf_op jit(solution)/shard_map/all_to_all | solution.py:692
  132.2 14.2 %collective-permute-start.19 = (bf16[272,768]{1,0:T(8,128)(2,1)S(1)}, bf16[272,768]{1,0:T(8,128)(2,1)}, u32[]{:S(2)}, u32[]{:S(2)}) collective-permute-start(bf16[272,768]{1,0:T(8,128)(2,1)S(1)} %pad_maximum_fusion.8.refs_0_), channel_id=1, source_target_pairs={{0,2},{2,0},{1,3},{3,1},{4,6},{6,4},{5,7},{7,5},{8,10},{10,8},{9,1... | collective-permute-start | bytes 1253384 | tf_op jit(solution)/shard_map/ppermute | solution.py:511
  133.5 15.5 %collective-permute-start.20 = (bf16[272,768]{1,0:T(8,128)(2,1)S(1)}, bf16[272,768]{1,0:T(8,128)(2,1)}, u32[]{:S(2)}, u32[]{:S(2)}) collective-permute-start(bf16[272,768]{1,0:T(8,128)(2,1)S(1)} %pad_maximum_fusion.8.refs_0_), channel_id=1, source_target_pairs={{0,4},{4,0},{1,5},{5,1},{2,6},{6,2},{3,7},{7,3},{8,12},{12,8},{9,1... | collective-permute-start | bytes 1253384 | tf_op jit(solution)/shard_map/ppermute | solution.py:511
  134.6 20.0 %collective-permute-start.21 = (bf16[272,768]{1,0:T(8,128)(2,1)S(1)}, bf16[272,768]{1,0:T(8,128)(2,1)}, u32[]{:S(2)}, u32[]{:S(2)}) collective-permute-start(bf16[272,768]{1,0:T(8,128)(2,1)S(1)} %pad_maximum_fusion.8.refs_0_), channel_id=1, source_target_pairs={{0,6},{2,4},{4,2},{6,0},{1,7},{3,5},{5,3},{7,1},{8,14},{10,12},{12... | collective-permute-start | bytes 1253384 | tf_op jit(solution)/shard_map/ppermute | solution.py:515
  140.1 15.0 %collective-permute-start.22 = (bf16[272,768]{1,0:T(8,128)(2,1)S(1)}, bf16[272,768]{1,0:T(8,128)(2,1)S(1)}, u32[]{:S(2)}, u32[]{:S(2)}) collective-permute-start(bf16[272,768]{1,0:T(8,128)(2,1)S(1)} %pad_maximum_fusion.8.refs_0_), channel_id=1, source_target_pairs={{0,1},{1,0},{2,3},{3,2},{4,5},{5,4},{6,7},{7,6},{8,9},{9,8},{10,11... | collective-permute-start | bytes 1253384 | tf_op jit(solution)/shard_map/ppermute | solution.py:511
  146.4 9.4 %collective-permute-start.23 = (bf16[272,768]{1,0:T(8,128)(2,1)}, bf16[272,768]{1,0:T(8,128)(2,1)S(1)}, u32[]{:S(2)}, u32[]{:S(2)}) collective-permute-start(bf16[272,768]{1,0:T(8,128)(2,1)} %collective-permute-done.19.refs_1_), channel_id=1, source_target_pairs={{0,1},{1,0},{2,3},{3,2},{4,5},{5,4},{6,7},{7,6},{8,9},{9,8},{10,11... | collective-permute-start | bytes 1253384 | tf_op jit(solution)/shard_map/ppermute | solution.py:511
  149.0 7.2 %collective-permute-start.24 = (bf16[272,768]{1,0:T(8,128)(2,1)}, bf16[272,768]{1,0:T(8,128)(2,1)S(1)}, u32[]{:S(2)}, u32[]{:S(2)}) collective-permute-start(bf16[272,768]{1,0:T(8,128)(2,1)} %collective-permute-done.20.refs_2_), channel_id=1, source_target_pairs={{0,1},{1,0},{2,3},{3,2},{4,5},{5,4},{6,7},{7,6},{8,9},{9,8},{10,11... | collective-permute-start | bytes 1253384 | tf_op jit(solution)/shard_map/ppermute | solution.py:511
  154.6 2.2 collective-permute-start.25
  156.8 30.8 %collective-permute-start.26 = (bf16[2,256,768]{2,1,0:T(8,128)(2,1)S(1)}, bf16[2,256,768]{2,1,0:T(8,128)(2,1)S(1)}, u32[]{:S(2)}, u32[]{:S(2)}) collective-permute-start(bf16[2,256,768]{2,1,0:T(8,128)(2,1)S(1)} %pad_maximum_fusion.5.refs_0_), channel_id=1, source_target_pairs={{0,2},{2,0},{1,3},{3,1},{4,6},{6,4},{5,7},{7,5},{8,10},{10,8},{9,1... | collective-permute-start | bytes 2359304 | tf_op jit(solution)/shard_map/ppermute | solution.py:511
  157.1 30.5 %collective-permute-start.27 = (bf16[2,256,768]{2,1,0:T(8,128)(2,1)S(1)}, bf16[2,256,768]{2,1,0:T(8,128)(2,1)S(1)}, u32[]{:S(2)}, u32[]{:S(2)}) collective-permute-start(bf16[2,256,768]{2,1,0:T(8,128)(2,1)S(1)} %pad_maximum_fusion.6.refs_1_), channel_id=1, source_target_pairs={{0,4},{4,0},{1,5},{5,1},{2,6},{6,2},{3,7},{7,3},{8,12},{12,8},{9,1... | collective-permute-start | bytes 2359304 | tf_op jit(solution)/shard_map/ppermute | solution.py:511
  188.4 10.6 %collective-permute-start.28 = (bf16[4,272,768]{2,1,0:T(8,128)(2,1)}, bf16[4,272,768]{2,1,0:T(8,128)(2,1)}, u32[]{:S(2)}, u32[]{:S(2)}) collective-permute-start(bf16[4,272,768]{2,1,0:T(8,128)(2,1)} %get-tuple-element.163), channel_id=1, source_target_pairs={{0,1},{1,0},{2,3},{3,2},{4,5},{5,4},{6,7},{7,6},{8,9},{9,8},{10,11... | collective-permute-start | bytes 5013512 | tf_op jit(solution)/shard_map/ppermute | solution.py:511
  201.0 20.1 %collective-permute-start.31 = (bf16[272,768]{1,0:T(8,128)(2,1)S(1)}, bf16[272,768]{1,0:T(8,128)(2,1)S(1)}, u32[]{:S(2)}, u32[]{:S(2)}) collective-permute-start(bf16[272,768]{1,0:T(8,128)(2,1)S(1)} %get-tuple-element.170), channel_id=1, source_target_pairs={{0,6},{2,4},{4,2},{6,0},{1,7},{3,5},{5,3},{7,1},{8,14},{10,12},{12... | collective-permute-start | bytes 1253384 | tf_op jit(solution)/shard_map/ppermute | solution.py:515
  202.2 20.3 %collective-permute-start.30 = (bf16[272,768]{1,0:T(8,128)(2,1)S(1)}, bf16[272,768]{1,0:T(8,128)(2,1)S(1)}, u32[]{:S(2)}, u32[]{:S(2)}) collective-permute-start(bf16[272,768]{1,0:T(8,128)(2,1)S(1)} %get-tuple-element.169), channel_id=1, source_target_pairs={{0,4},{4,0},{1,5},{5,1},{2,6},{6,2},{3,7},{7,3},{8,12},{12,8},{9,1... | collective-permute-start | bytes 1253384 | tf_op jit(solution)/shard_map/ppermute | solution.py:511
  203.4 19.1 %collective-permute-start.29 = (bf16[272,768]{1,0:T(8,128)(2,1)S(1)}, bf16[272,768]{1,0:T(8,128)(2,1)S(1)}, u32[]{:S(2)}, u32[]{:S(2)}) collective-permute-start(bf16[272,768]{1,0:T(8,128)(2,1)S(1)} %get-tuple-element.168), channel_id=1, source_target_pairs={{0,2},{2,0},{1,3},{3,1},{4,6},{6,4},{5,7},{7,5},{8,10},{10,8},{9,1... | collective-permute-start | bytes 1253384 | tf_op jit(solution)/shard_map/ppermute | solution.py:511
  226.6 16.8 %collective-permute-start.33 = (bf16[768,384]{0,1:T(8,128)(2,1)}, bf16[768,384]{0,1:T(8,128)(2,1)}, u32[]{:S(2)}, u32[]{:S(2)}) collective-permute-start(bf16[768,384]{0,1:T(8,128)(2,1)} %convolution_convert_fusion.2), channel_id=1, source_target_pairs={{0,1},{1,0},{2,3},{3,2},{4,5},{5,4},{6,7},{7,6},{8,9},{9,8},{10,11... | collective-permute-start | bytes 1769480 | tf_op jit(solution)/shard_map/ppermute | solution.py:511
  229.8 42.3 %collective-permute-start.34 = (bf16[192,3072]{1,0:T(8,128)(2,1)}, bf16[192,3072]{1,0:T(8,128)(2,1)}, u32[]{:S(2)}, u32[]{:S(2)}) collective-permute-start(bf16[192,3072]{1,0:T(8,128)(2,1)} %dynamic-slice_bitcast_fusion.5), channel_id=1, source_target_pairs={{0,8},{24,16},{1,9},{25,17},{2,10},{26,18},{3,11},{27,19},{4,12},{... | collective-permute-start | bytes 3538952 | tf_op jit(solution)/shard_map/ppermute | solution.py:555
  234.4 43.8 %all-to-all-start.2 = ((bf16[16,64,256]{2,1,0:T(8,128)(2,1)}), bf16[16,64,256]{2,1,0:T(8,128)(2,1)}, u32[]{:S(2)}, u32[]{:S(2)}) async-start(bf16[16,64,256]{2,1,0:T(8,128)(2,1)} %copy-done.8), calls=%async_computation.2 | async-start | bytes 1048576 | tf_op jit(solution)/shard_map/all_to_all | solution.py:692
  241.8 33.8 %collective-permute-start.32 = (bf16[4,256,768]{2,1,0:T(8,128)(2,1)}, bf16[4,256,768]{2,1,0:T(8,128)(2,1)}, u32[]{:S(2)}, u32[]{:S(2)}) collective-permute-start(bf16[4,256,768]{2,1,0:T(8,128)(2,1)} %convolution_convert_fusion), channel_id=1, source_target_pairs={{0,1},{1,0},{2,3},{3,2},{4,5},{5,4},{6,7},{7,6},{8,9},{9,8},{10,11... | collective-permute-start | bytes 4718600 | tf_op jit(solution)/shard_map/ppermute | solution.py:511
  250.1 21.9 %collective-permute-start.35 = (bf16[192,512]{1,0:T(8,128)(2,1)S(1)}, bf16[192,512]{1,0:T(8,128)(2,1)S(1)}, u32[]{:S(2)}, u32[]{:S(2)}) collective-permute-start(bf16[192,512]{1,0:T(8,128)(2,1)S(1)} %get-tuple-element.334), channel_id=1, source_target_pairs={{0,8},{24,16},{1,9},{25,17},{2,10},{26,18},{3,11},{27,19},{4,12},{... | collective-permute-start | bytes 589832 | tf_op jit(solution)/shard_map/ppermute | solution.py:555
  278.2 42.5 %collective-permute-start.36 = (bf16[2,2,256,768]{3,2,1,0:T(8,128)(2,1)}, bf16[2,2,256,768]{3,2,1,0:T(8,128)(2,1)S(1)}, u32[]{:S(2)}, u32[]{:S(2)}) collective-permute-start(bf16[2,2,256,768]{3,2,1,0:T(8,128)(2,1)} %pad_maximum_fusion.1), channel_id=1, source_target_pairs={{0,4},{4,0},{1,5},{5,1},{2,6},{6,2},{3,7},{7,3},{8,12},{12,8},{9,1... | collective-permute-start | bytes 4718600 | tf_op jit(solution)/shard_map/ppermute | solution.py:511
  278.6 42.1 %collective-permute-start.37 = (bf16[2,2,256,768]{3,2,1,0:T(8,128)(2,1)}, bf16[2,2,256,768]{3,2,1,0:T(8,128)(2,1)S(1)}, u32[]{:S(2)}, u32[]{:S(2)}) collective-permute-start(bf16[2,2,256,768]{3,2,1,0:T(8,128)(2,1)} %pad_maximum_fusion.2), channel_id=1, source_target_pairs={{0,2},{2,0},{1,3},{3,1},{4,6},{6,4},{5,7},{7,5},{8,10},{10,8},{9,1... | collective-permute-start | bytes 4718600 | tf_op jit(solution)/shard_map/ppermute | solution.py:511
  279.7 40.9 %collective-permute-start.38 = (bf16[192,3584]{1,0:T(8,128)(2,1)}, bf16[192,3584]{1,0:T(8,128)(2,1)}, u32[]{:S(2)}, u32[]{:S(2)}) collective-permute-start(bf16[192,3584]{1,0:T(8,128)(2,1)} %get-tuple-element.189), channel_id=1, source_target_pairs={{0,8},{8,16},{1,9},{9,17},{2,10},{10,18},{3,11},{11,19},{4,12},{12... | collective-permute-start | bytes 4128776 | tf_op jit(solution)/shard_map/ppermute | solution.py:559
  281.0 39.6 %collective-permute-start.39 = (bf16[192,3584]{1,0:T(8,128)(2,1)}, bf16[192,3584]{1,0:T(8,128)(2,1)}, u32[]{:S(2)}, u32[]{:S(2)}) collective-permute-start(bf16[192,3584]{1,0:T(8,128)(2,1)} %get-tuple-element.190), channel_id=1, source_target_pairs={{24,16},{16,8},{25,17},{17,9},{26,18},{18,10},{27,19},{19,11},{28,... | collective-permute-start | bytes 4128776 | tf_op jit(solution)/shard_map/ppermute | solution.py:560
  320.7 9.8 %collective-permute-start.40 = (bf16[5,128,256]{2,1,0:T(8,128)(2,1)}, bf16[5,128,256]{2,1,0:T(8,128)(2,1)S(1)}, u32[]{:S(2)}, u32[]{:S(2)}) collective-permute-start(bf16[5,128,256]{2,1,0:T(8,128)(2,1)} %get-tuple-element.194), channel_id=1, source_target_pairs={{0,1},{1,0},{2,3},{3,2},{4,5},{5,4},{6,7},{7,6},{8,9},{9,8},{10,11... | collective-permute-start | bytes 983048 | tf_op jit(solution)/shard_map/ppermute | solution.py:511
  330.4 59.8 %copy-start.106 = (s32[16]{0:T(128)S(1)}, s32[16]{0:T(128)}, u32[]{:S(2)}) copy-start(s32[16]{0:T(128)} %constant.201.clone) | copy-start | bytes 196
  330.5 59.9 %copy-start.85 = (f32[256,3]{0,1:T(4,128)S(1)}, f32[256,3]{0,1:T(4,128)}, u32[]{:S(2)}) copy-start(f32[256,3]{0,1:T(4,128)} %copy-done.84) | copy-start | bytes 9220
  330.5 42.1 %collective-permute-start.41 = (bf16[192,3584]{1,0:T(8,128)(2,1)}, bf16[192,3584]{1,0:T(8,128)(2,1)}, u32[]{:S(2)}, u32[]{:S(2)}) collective-permute-start(bf16[192,3584]{1,0:T(8,128)(2,1)} %add_convert_fusion.2), channel_id=1, source_target_pairs={{0,8},{8,16},{16,24},{1,9},{9,17},{17,25},{2,10},{10,18},{18,26},{... | collective-permute-start | bytes 4128776 | tf_op jit(solution)/shard_map/ppermute | solution.py:559
  332.6 40.0 %collective-permute-start.42 = (bf16[192,3584]{1,0:T(8,128)(2,1)S(1)}, bf16[192,3584]{1,0:T(8,128)(2,1)}, u32[]{:S(2)}, u32[]{:S(2)}) collective-permute-start(bf16[192,3584]{1,0:T(8,128)(2,1)S(1)} %add_convert_fusion.1), channel_id=1, source_target_pairs={{24,16},{16,8},{8,0},{25,17},{17,9},{9,1},{26,18},{18,10},{10,2},{... | collective-permute-start | bytes 4128776 | tf_op jit(solution)/shard_map/ppermute | solution.py:560
  335.8 36.8 %collective-permute-start.43 = (bf16[256,768]{1,0:T(8,128)(2,1)S(1)}, bf16[256,768]{1,0:T(8,128)(2,1)S(1)}, u32[]{:S(2)}, u32[]{:S(2)}) collective-permute-start(bf16[256,768]{1,0:T(8,128)(2,1)S(1)} %copy-done.64), channel_id=1, source_target_pairs={{0,2},{2,0},{1,3},{3,1},{4,6},{6,4},{5,7},{7,5},{8,10},{10,8},{9,1... | collective-permute-start | bytes 1179656 | tf_op jit(solution)/shard_map/ppermute | solution.py:511
  336.2 36.4 %collective-permute-start.44 = (bf16[256,768]{1,0:T(8,128)(2,1)S(1)}, bf16[256,768]{1,0:T(8,128)(2,1)S(1)}, u32[]{:S(2)}, u32[]{:S(2)}) collective-permute-start(bf16[256,768]{1,0:T(8,128)(2,1)S(1)} %copy-done.63), channel_id=1, source_target_pairs={{0,4},{4,0},{1,5},{5,1},{2,6},{6,2},{3,7},{7,3},{8,12},{12,8},{9,1... | collective-permute-start | bytes 1179656 | tf_op jit(solution)/shard_map/ppermute | solution.py:511
  337.3 35.3 %collective-permute-start.45 = (bf16[256,768]{1,0:T(8,128)(2,1)S(1)}, bf16[256,768]{1,0:T(8,128)(2,1)S(1)}, u32[]{:S(2)}, u32[]{:S(2)}) collective-permute-start(bf16[256,768]{1,0:T(8,128)(2,1)S(1)} %copy-done.62), channel_id=1, source_target_pairs={{0,6},{2,4},{4,2},{6,0},{1,7},{3,5},{5,3},{7,1},{8,14},{10,12},{12... | collective-permute-start | bytes 1179656 | tf_op jit(solution)/shard_map/ppermute | solution.py:515
  373.6 18.4 %collective-permute-start.46 = (bf16[11,128,256]{2,1,0:T(8,128)(2,1)}, bf16[11,128,256]{2,1,0:T(8,128)(2,1)}, u32[]{:S(2)}, u32[]{:S(2)}) collective-permute-start(bf16[11,128,256]{2,1,0:T(8,128)(2,1)} %get-tuple-element.206), channel_id=1, source_target_pairs={{0,1},{1,0},{2,3},{3,2},{4,5},{5,4},{6,7},{7,6},{8,9},{9,8},{10,11... | collective-permute-start | bytes 2162696 | tf_op jit(solution)/shard_map/ppermute | solution.py:511
  403.3 60.7 %all-to-all-start.3 = ((bf16[16,240,256]{2,1,0:T(8,128)(2,1)}), bf16[16,240,256]{2,1,0:T(8,128)(2,1)}, u32[]{:S(2)}, u32[]{:S(2)}) async-start(bf16[16,240,256]{2,1,0:T(8,128)(2,1)} %head_grad.1), calls=%async_computation.3 | async-start | bytes 3932160 | tf_op jit(solution)/shard_map/all_to_all | solution.py:692
  409.2 25.2 %collective-permute-start.47 = (f32[256,8]{0,1:T(8,128)S(1)}, f32[256,8]{0,1:T(8,128)S(1)}, u32[]{:S(2)}, u32[]{:S(2)}) collective-permute-start(f32[256,8]{0,1:T(8,128)S(1)} %bitcast.236), channel_id=1, source_target_pairs={{0,1},{1,0},{2,3},{3,2},{4,5},{5,4},{6,7},{7,6},{8,9},{9,8},{10,11... | collective-permute-start | bytes 24584 | tf_op jit(solution)/shard_map/ppermute | solution.py:511
  415.6 18.8 %collective-permute-start.51 = (bf16[48,3584]{1,0:T(8,128)(2,1)}, bf16[48,3584]{1,0:T(8,128)(2,1)}, u32[]{:S(2)}, u32[]{:S(2)}) collective-permute-start(bf16[48,3584]{1,0:T(8,128)(2,1)} %get-tuple-element.320), channel_id=1, source_target_pairs={{0,6},{2,4},{4,2},{6,0},{1,7},{3,5},{5,3},{7,1},{8,14},{10,12},{12... | collective-permute-start | bytes 1032200 | tf_op jit(solution)/shard_map/ppermute | solution.py:515
  417.7 25.5 %collective-permute-start.50 = (bf16[48,3584]{1,0:T(8,128)(2,1)}, bf16[48,3584]{1,0:T(8,128)(2,1)}, u32[]{:S(2)}, u32[]{:S(2)}) collective-permute-start(bf16[48,3584]{1,0:T(8,128)(2,1)} %get-tuple-element.321), channel_id=1, source_target_pairs={{0,4},{4,0},{1,5},{5,1},{2,6},{6,2},{3,7},{7,3},{8,12},{12,8},{9,1... | collective-permute-start | bytes 1032200 | tf_op jit(solution)/shard_map/ppermute | solution.py:511
  417.9 37.2 %collective-permute-start.49 = (bf16[48,3584]{1,0:T(8,128)(2,1)}, bf16[48,3584]{1,0:T(8,128)(2,1)}, u32[]{:S(2)}, u32[]{:S(2)}) collective-permute-start(bf16[48,3584]{1,0:T(8,128)(2,1)} %get-tuple-element.322), channel_id=1, source_target_pairs={{0,2},{2,0},{1,3},{3,1},{4,6},{6,4},{5,7},{7,5},{8,10},{10,8},{9,1... | collective-permute-start | bytes 1032200 | tf_op jit(solution)/shard_map/ppermute | solution.py:511
  433.5 29.7 %collective-permute-start.48 = (bf16[256,768]{1,0:T(8,128)(2,1)S(1)}, bf16[256,768]{1,0:T(8,128)(2,1)S(1)}, u32[]{:S(2)}, u32[]{:S(2)}) collective-permute-start(bf16[256,768]{1,0:T(8,128)(2,1)S(1)} %copy-done.65), channel_id=1, source_target_pairs={{0,1},{1,0},{2,3},{3,2},{4,5},{5,4},{6,7},{7,6},{8,9},{9,8},{10,11... | collective-permute-start | bytes 1179656 | tf_op jit(solution)/shard_map/ppermute | solution.py:511
  460.1 3.1 collective-permute-start.52
  471.1 7.2 %collective-permute-start.53 = (f32[256,768]{1,0:T(8,128)}, f32[256,768]{1,0:T(8,128)}, u32[]{:S(2)}, u32[]{:S(2)}) collective-permute-start(f32[256,768]{1,0:T(8,128)} %get-tuple-element.293), channel_id=1, source_target_pairs={{0,1},{1,0},{2,3},{3,2},{4,5},{5,4},{6,7},{7,6},{8,9},{9,8},{10,11... | collective-permute-start | bytes 2359304 | tf_op jit(solution)/shard_map/ppermute | solution.py:511
  472.1 1.5 collective-permute-start.54
  475.3 2.4 collective-permute-start.55
  (109 other events, 774.5 us)
